TPU v7x, 768 devices: a whole 4x8x12 slice. The times are simulated.
768 devices in a mesh: gx: 6 (over z_hi, core), gy: 8 (over y), gz: 16 (over z_lo, x).
Axes of the slice: x: 4, y: 8, z: 12 (z_hi: 3, z_lo: 4; z = z_hi * 4 + z_lo), core: 2. Of those that a mesh axis runs over, the one named last changes fastest.
Arguments:
- wavefunctions: bfloat16 [42, 56, 112, 128], P('gx', 'gy', 'gz'), may hold values from -8 to 8, as said below
- cell_hamiltonian: bfloat16 [6, 8, 16, 343, 343], P('gx', 'gy', 'gz'), may hold values from -0.15625 to 0.15625
- projectors: bfloat16 [6, 8, 16, 8, 18, 343], P('gx', 'gy', 'gz'), may hold values from -0.3125 to 0.3125
- atom_species: int32 [12, 16, 32], P('gx', 'gy', 'gz'), may hold values from 0 to 2, as said below
- coupling: float32 [2, 18, 18], replicated, may hold values from -0.875 to 0.875
Outputs:
- filtered: bfloat16 [42, 56, 112, 128], P('gx', 'gy', 'gz')
Inputs may be any that keep to these rules, and one draw needn't show every extreme that they name: `wavefunctions`: entries that stand for the same node in neighbouring blocks are equal. `atom_species`: entries that stand for the same vertex in neighbouring blocks are equal; 0 marks a vertex without an atom, k an atom of species k.
All inputs are finite; a program needn't handle non-finite values.
Results may differ from a plain program's by a relative error of at most 0.008.
Values sent between devices are 32-bit elements; how exact they have to be, the bound alone decides.
No kernel may reach another device: no remote copies, remote signals or barrier semaphores. Data moves between devices by JAX's collectives and lax.ppermute only.
A program may use at most 32 MiB of HBM per device.

v0:
```python
import jax
import jax.numpy as jnp
from jax import lax
from jax.sharding import PartitionSpec as P

PDEG = 6
ORDER = 4


CENTER = 0.1
HALF = 2.0


def with_halo(cells, sides, width):
    for axis, dim in sides:
        count = lax.axis_size(axis)
        head = lax.slice_in_dim(cells, 0, width, axis=dim)
        tail = lax.slice_in_dim(cells, cells.shape[dim] - width, cells.shape[dim], axis=dim)
        cells = jnp.concatenate(
            [
                lax.ppermute(tail, axis, [(i, (i + 1) % count) for i in range(count)]),
                cells,
                lax.ppermute(head, axis, [((i + 1) % count, i) for i in range(count)]),
            ],
            axis=dim,
        )
    return cells


def fold_rims(padded, dimension):
    length = padded.shape[dimension]
    lower = lax.slice_in_dim(padded, 0, 1, axis=dimension)
    upper = lax.slice_in_dim(padded, length - 1, length, axis=dimension)
    first_row = lax.slice_in_dim(padded, 1, 2, axis=dimension) + lower
    middle = lax.slice_in_dim(padded, 2, length - 2, axis=dimension)
    last_row = lax.slice_in_dim(padded, length - 2, length - 1, axis=dimension) + upper
    return jnp.concatenate([first_row, middle, last_row], axis=dimension)


def fold_all(padded):
    return fold_rims(fold_rims(fold_rims(padded, 0), 1), 2)


def windows_of(values, dimension):
    slices = [values]
    return jnp.stack(slices, axis=dimension)


def deposit(blocks, dimension):
    single = lax.index_in_dim(blocks, 0, axis=dimension, keepdims=False)
    return single


def split_cells(nodal, degree, counts):
    stacked = windows_of(nodal, 0)
    stacked = windows_of(stacked, 2)
    stacked = windows_of(stacked, 4)
    stacked = jnp.transpose(stacked, (0, 2, 4, 1, 3, 5, 6))
    return stacked.reshape(counts[0] * counts[1] * counts[2], (degree + 1) ** 3, nodal.shape[3])


def join_cells(terms, degree, counts, width):
    side = degree + 1
    blocks = terms.reshape(counts[0], counts[1], counts[2], side, side, side, width)
    blocks = jnp.transpose(blocks, (0, 3, 1, 4, 2, 5, 6))
    blocks = deposit(blocks, 4)
    blocks = deposit(blocks, 2)
    return deposit(blocks, 0)


def local(wavefunctions, cell_hamiltonian, projectors, atom_species, coupling):
    counts = cell_hamiltonian.shape[:3]
    cell_count = counts[0] * counts[1] * counts[2]
    node_count = cell_hamiltonian.shape[3]
    width = wavefunctions.shape[3]
    nproj = projectors.shape[4]
    hamiltonian = cell_hamiltonian.reshape(cell_count, node_count, node_count)
    betas = projectors.reshape(cell_count, 8, nproj, node_count)
    kinds = jnp.arange(1, coupling.shape[0] + 1, dtype=jnp.int32)
    species_mask = (atom_species[..., None] == kinds).astype(jnp.float32)
    vertex_coupling = jnp.einsum(
        "xyzs,spq->xyzpq", species_mask, coupling, precision=lax.Precision.HIGHEST
    )
    current = wavefunctions
    previous = wavefunctions
    for step in range(ORDER):
        cells = split_cells(current, PDEG, counts)
        local_terms = jnp.einsum(
            "cnm,cmw->cnw", hamiltonian, cells, preferred_element_type=jnp.float32
        )
        partial_value = jnp.einsum(
            "ckpn,cnw->ckpw", betas, cells, preferred_element_type=jnp.float32
        )
        partial_value = partial_value.reshape(
            counts[0], counts[1], counts[2], 2, 2, 2, nproj, width
        )
        vertex_sums = None
        for corner_x in range(2):
            for corner_y in range(2):
                for corner_z in range(2):
                    placed = jnp.pad(
                        partial_value[:, :, :, corner_x, corner_y, corner_z],
                        (
                            (corner_x, 1 - corner_x),
                            (corner_y, 1 - corner_y),
                            (corner_z, 1 - corner_z),
                            (0, 0),
                            (0, 0),
                        ),
                    )
                    vertex_sums = placed if vertex_sums is None else vertex_sums + placed
        vertex_rims = with_halo(vertex_sums, (("gx", 0), ("gy", 1), ("gz", 2)), 1)
        correlations = fold_all(vertex_rims)
        coefficients = jnp.einsum(
            "xyzpq,xyzqw->xyzpw", vertex_coupling, correlations, precision=lax.Precision.HIGHEST
        ).astype(jnp.bfloat16)
        corner_list = []
        for corner_x in range(2):
            for corner_y in range(2):
                for corner_z in range(2):
                    corner_list.append(
                        coefficients[
                            corner_x : corner_x + counts[0],
                            corner_y : corner_y + counts[1],
                            corner_z : corner_z + counts[2],
                        ]
                    )
        corner_coefs = jnp.stack(corner_list, axis=3).reshape(cell_count, 8, nproj, width)
        projector_terms = jnp.einsum(
            "ckpn,ckpw->cnw", betas, corner_coefs, preferred_element_type=jnp.float32
        )
        nodal_terms = join_cells(local_terms + projector_terms, PDEG, counts, width)
        node_rims = with_halo(nodal_terms, (("gx", 0), ("gy", 1), ("gz", 2)), 1)
        applied = fold_all(node_rims)
        current_wide = current.astype(jnp.float32)
        if step == 0:
            updated = (applied - CENTER * current_wide) / HALF
        else:
            updated = 2.0 * (applied - CENTER * current_wide) / HALF - previous.astype(jnp.float32)
        previous = current
        current = updated.astype(jnp.bfloat16)
    return current


def solution(mesh):
    placed = (
        P("gx", "gy", "gz", None),
        P("gx", "gy", "gz", None, None),
        P("gx", "gy", "gz", None, None, None),
        P("gx", "gy", "gz"),
        P(),
    )
    return jax.shard_map(
        local, mesh=mesh, in_specs=placed, out_specs=P("gx", "gy", "gz", None), check_vma=False
    )
```

profile of v0, /device:TPU:1, one launch (start us, length us, event | category | flops | bytes accessed | tf_op | source)
XLA Modules:
  0.0 293.2 jit_solution(15593142848491809642)
XLA Ops:
  1.3 12.0 %collective-permute-start = (f32[1,2,2,18,128]{4,3,2,1,0:T(8,128)S(1)}, f32[1,2,2,18,128]{4,3,2,1,0:T(8,128)S(1)}, u32[]{:S(2)}, u32[]{:S(2)}) collective-permute-start(f32[1,2,2,18,128]{4,3,2,1,0:T(8,128)S(1)} %get-tuple-element.115), channel_id=1, source_target_pairs={{0,128},{128,256},{256,384},{384,512},{512,640},{640,0},{1,129},{1... | collective-permute-start | bytes 110600 | tf_op jit(solution)/shard_map/ppermute | solution.py:21
  15.7 7.1 %collective-permute-done.1 = f32[1,2,2,18,128]{4,3,2,1,0:T(8,128)S(1)} collective-permute-done((f32[1,2,2,18,128]{4,3,2,1,0:T(8,128)S(1)}, f32[1,2,2,18,128]{4,3,2,1,0:T(8,128)S(1)}, u32[]{:S(2)}, u32[]{:S(2)}) %collective-permute-start.1) | collective-permute-done | bytes 36896 | tf_op jit(solution)/shard_map/ppermute | solution.py:23
  26.0 3.8 %collective-permute-start.3 = (f32[4,1,2,18,128]{4,3,2,1,0:T(8,128)S(1)}, f32[4,1,2,18,128]{4,3,2,1,0:T(8,128)S(1)}, u32[]{:S(2)}, u32[]{:S(2)}) collective-permute-start(f32[4,1,2,18,128]{4,3,2,1,0:T(8,128)S(1)} %get-tuple-element.76), channel_id=1, source_target_pairs={{16,0},{32,16},{48,32},{64,48},{80,64},{96,80},{112,96},{0,112},{1... | collective-permute-start | bytes 221192 | tf_op jit(solution)/shard_map/ppermute | solution.py:23
  34.6 8.2 %collective-permute-start.5 = (f32[4,4,1,18,128]{4,3,2,1,0:T(8,128)S(1)}, f32[4,4,1,18,128]{4,3,2,1,0:T(8,128)S(1)}, u32[]{:S(2)}, u32[]{:S(2)}) collective-permute-start(f32[4,4,1,18,128]{4,3,2,1,0:T(8,128)S(1)} %get-tuple-element.44), channel_id=1, source_target_pairs={{1,0},{2,1},{3,2},{4,3},{5,4},{6,5},{7,6},{8,7},{9,8},{10,9},{11,1... | collective-permute-start | bytes 442376 | tf_op jit(solution)/shard_map/ppermute | solution.py:23
  53.6 6.9 %collective-permute-done.7 = f32[1,7,7,128]{3,0,2,1:T(1,128)S(1)} collective-permute-done((f32[1,7,7,128]{3,0,2,1:T(1,128)S(1)}, f32[1,7,7,128]{3,0,2,1:T(1,128)S(1)}, u32[]{:S(2)}, u32[]{:S(2)}) %collective-permute-start.7) | collective-permute-done | bytes 25120 | tf_op jit(solution)/shard_map/ppermute | solution.py:23
  71.0 7.9 %collective-permute-start.11 = (f32[9,9,1,128]{3,2,1,0:T(1,128)S(1)}, f32[9,9,1,128]{3,2,1,0:T(1,128)S(1)}, u32[]{:S(2)}, u32[]{:S(2)}) collective-permute-start(f32[9,9,1,128]{3,2,1,0:T(1,128)S(1)} %get-tuple-element.52), channel_id=1, source_target_pairs={{1,0},{2,1},{3,2},{4,3},{5,4},{6,5},{7,6},{8,7},{9,8},{10,9},{11,1... | collective-permute-start | bytes 124424 | tf_op jit(solution)/shard_map/ppermute | solution.py:23
  80.9 3.9 %collective-permute-start.12 = (f32[1,2,2,18,128]{4,3,2,1,0:T(8,128)S(1)}, f32[1,2,2,18,128]{4,3,2,1,0:T(8,128)S(1)}, u32[]{:S(2)}, u32[]{:S(2)}) collective-permute-start(f32[1,2,2,18,128]{4,3,2,1,0:T(8,128)S(1)} %get-tuple-element.105), channel_id=1, source_target_pairs={{0,128},{128,256},{256,384},{384,512},{512,640},{640,0},{1,129},{1... | collective-permute-start | bytes 110600 | tf_op jit(solution)/shard_map/ppermute | solution.py:21
  86.8 7.6 %collective-permute-done.13 = f32[1,2,2,18,128]{4,3,2,1,0:T(8,128)S(1)} collective-permute-done((f32[1,2,2,18,128]{4,3,2,1,0:T(8,128)S(1)}, f32[1,2,2,18,128]{4,3,2,1,0:T(8,128)S(1)}, u32[]{:S(2)}, u32[]{:S(2)}) %collective-permute-start.13) | collective-permute-done | bytes 36896 | tf_op jit(solution)/shard_map/ppermute | solution.py:23
  94.4 5.1 %collective-permute-start.14 = (f32[4,1,2,18,128]{4,3,2,1,0:T(8,128)S(1)}, f32[4,1,2,18,128]{4,3,2,1,0:T(8,128)S(1)}, u32[]{:S(2)}, u32[]{:S(2)}) collective-permute-start(f32[4,1,2,18,128]{4,3,2,1,0:T(8,128)S(1)} %get-tuple-element.71), channel_id=1, source_target_pairs={{0,16},{16,32},{32,48},{48,64},{64,80},{80,96},{96,112},{112,0},{1... | collective-permute-start | bytes 221192 | tf_op jit(solution)/shard_map/ppermute | solution.py:21
  107.2 7.3 %collective-permute-start.17 = (f32[4,4,1,18,128]{4,3,2,1,0:T(8,128)S(1)}, f32[4,4,1,18,128]{4,3,2,1,0:T(8,128)S(1)}, u32[]{:S(2)}, u32[]{:S(2)}) collective-permute-start(f32[4,4,1,18,128]{4,3,2,1,0:T(8,128)S(1)} %get-tuple-element.40), channel_id=1, source_target_pairs={{1,0},{2,1},{3,2},{4,3},{5,4},{6,5},{7,6},{8,7},{9,8},{10,9},{11,1... | collective-permute-start | bytes 442376 | tf_op jit(solution)/shard_map/ppermute | solution.py:23
  124.6 6.8 %collective-permute-done.19 = f32[1,7,7,128]{3,0,2,1:T(1,128)S(1)} collective-permute-done((f32[1,7,7,128]{3,0,2,1:T(1,128)S(1)}, f32[1,7,7,128]{3,0,2,1:T(1,128)S(1)}, u32[]{:S(2)}, u32[]{:S(2)}) %collective-permute-start.19) | collective-permute-done | bytes 25120 | tf_op jit(solution)/shard_map/ppermute | solution.py:23
  141.8 8.0 %collective-permute-start.23 = (f32[9,9,1,128]{3,2,1,0:T(1,128)S(1)}, f32[9,9,1,128]{3,2,1,0:T(1,128)S(1)}, u32[]{:S(2)}, u32[]{:S(2)}) collective-permute-start(f32[9,9,1,128]{3,2,1,0:T(1,128)S(1)} %get-tuple-element.50), channel_id=1, source_target_pairs={{1,0},{2,1},{3,2},{4,3},{5,4},{6,5},{7,6},{8,7},{9,8},{10,9},{11,1... | collective-permute-start | bytes 124424 | tf_op jit(solution)/shard_map/ppermute | solution.py:23
  151.8 4.2 %collective-permute-start.24 = (f32[1,2,2,18,128]{4,3,2,1,0:T(8,128)S(1)}, f32[1,2,2,18,128]{4,3,2,1,0:T(8,128)S(1)}, u32[]{:S(2)}, u32[]{:S(2)}) collective-permute-start(f32[1,2,2,18,128]{4,3,2,1,0:T(8,128)S(1)} %get-tuple-element.95), channel_id=1, source_target_pairs={{0,128},{128,256},{256,384},{384,512},{512,640},{640,0},{1,129},{1... | collective-permute-start | bytes 110600 | tf_op jit(solution)/shard_map/ppermute | solution.py:21
  157.9 7.4 %collective-permute-done.25 = f32[1,2,2,18,128]{4,3,2,1,0:T(8,128)S(1)} collective-permute-done((f32[1,2,2,18,128]{4,3,2,1,0:T(8,128)S(1)}, f32[1,2,2,18,128]{4,3,2,1,0:T(8,128)S(1)}, u32[]{:S(2)}, u32[]{:S(2)}) %collective-permute-start.25) | collective-permute-done | bytes 36896 | tf_op jit(solution)/shard_map/ppermute | solution.py:23
  168.2 3.6 %collective-permute-start.27 = (f32[4,1,2,18,128]{4,3,2,1,0:T(8,128)S(1)}, f32[4,1,2,18,128]{4,3,2,1,0:T(8,128)S(1)}, u32[]{:S(2)}, u32[]{:S(2)}) collective-permute-start(f32[4,1,2,18,128]{4,3,2,1,0:T(8,128)S(1)} %get-tuple-element.68), channel_id=1, source_target_pairs={{16,0},{32,16},{48,32},{64,48},{80,64},{96,80},{112,96},{0,112},{1... | collective-permute-start | bytes 221192 | tf_op jit(solution)/shard_map/ppermute | solution.py:23
  176.5 7.3 %collective-permute-start.29 = (f32[4,4,1,18,128]{4,3,2,1,0:T(8,128)S(1)}, f32[4,4,1,18,128]{4,3,2,1,0:T(8,128)S(1)}, u32[]{:S(2)}, u32[]{:S(2)}) collective-permute-start(f32[4,4,1,18,128]{4,3,2,1,0:T(8,128)S(1)} %get-tuple-element.36), channel_id=1, source_target_pairs={{1,0},{2,1},{3,2},{4,3},{5,4},{6,5},{7,6},{8,7},{9,8},{10,9},{11,1... | collective-permute-start | bytes 442376 | tf_op jit(solution)/shard_map/ppermute | solution.py:23
  194.0 6.4 %collective-permute-done.31 = f32[1,7,7,128]{3,0,2,1:T(1,128)S(1)} collective-permute-done((f32[1,7,7,128]{3,0,2,1:T(1,128)S(1)}, f32[1,7,7,128]{3,0,2,1:T(1,128)S(1)}, u32[]{:S(2)}, u32[]{:S(2)}) %collective-permute-start.31) | collective-permute-done | bytes 25120 | tf_op jit(solution)/shard_map/ppermute | solution.py:23
  203.6 3.7 %collective-permute-start.33 = (f32[9,1,7,128]{3,2,1,0:T(8,128)S(1)}, f32[9,1,7,128]{3,2,1,0:T(8,128)S(1)}, u32[]{:S(2)}, u32[]{:S(2)}) collective-permute-start(f32[9,1,7,128]{3,2,1,0:T(8,128)S(1)} %get-tuple-element.56), channel_id=1, source_target_pairs={{16,0},{32,16},{48,32},{64,48},{80,64},{96,80},{112,96},{0,112},{1... | collective-permute-start | bytes 96776 | tf_op jit(solution)/shard_map/ppermute | solution.py:23
  211.1 8.3 %collective-permute-start.35 = (f32[9,9,1,128]{3,2,1,0:T(1,128)S(1)}, f32[9,9,1,128]{3,2,1,0:T(1,128)S(1)}, u32[]{:S(2)}, u32[]{:S(2)}) collective-permute-start(f32[9,9,1,128]{3,2,1,0:T(1,128)S(1)} %get-tuple-element.48), channel_id=1, source_target_pairs={{1,0},{2,1},{3,2},{4,3},{5,4},{6,5},{7,6},{8,7},{9,8},{10,9},{11,1... | collective-permute-start | bytes 124424 | tf_op jit(solution)/shard_map/ppermute | solution.py:23
  221.3 5.0 %collective-permute-start.36 = (f32[1,2,2,18,128]{4,3,2,1,0:T(8,128)S(1)}, f32[1,2,2,18,128]{4,3,2,1,0:T(8,128)S(1)}, u32[]{:S(2)}, u32[]{:S(2)}) collective-permute-start(f32[1,2,2,18,128]{4,3,2,1,0:T(8,128)S(1)} %get-tuple-element.85), channel_id=1, source_target_pairs={{0,128},{128,256},{256,384},{384,512},{512,640},{640,0},{1,129},{1... | collective-permute-start | bytes 110600 | tf_op jit(solution)/shard_map/ppermute | solution.py:21
  228.3 7.4 %collective-permute-done.37 = f32[1,2,2,18,128]{4,3,2,1,0:T(8,128)S(1)} collective-permute-done((f32[1,2,2,18,128]{4,3,2,1,0:T(8,128)S(1)}, f32[1,2,2,18,128]{4,3,2,1,0:T(8,128)S(1)}, u32[]{:S(2)}, u32[]{:S(2)}) %collective-permute-start.37) | collective-permute-done | bytes 36896 | tf_op jit(solution)/shard_map/ppermute | solution.py:23
  248.0 7.9 %collective-permute-start.41 = (f32[4,4,1,18,128]{4,3,2,1,0:T(8,128)S(1)}, f32[4,4,1,18,128]{4,3,2,1,0:T(8,128)S(1)}, u32[]{:S(2)}, u32[]{:S(2)}) collective-permute-start(f32[4,4,1,18,128]{4,3,2,1,0:T(8,128)S(1)} %get-tuple-element.32), channel_id=1, source_target_pairs={{1,0},{2,1},{3,2},{4,3},{5,4},{6,5},{7,6},{8,7},{9,8},{10,9},{11,1... | collective-permute-start | bytes 442376 | tf_op jit(solution)/shard_map/ppermute | solution.py:23
  266.6 6.0 %collective-permute-done.43 = f32[1,7,7,128]{3,0,2,1:T(1,128)S(1)} collective-permute-done((f32[1,7,7,128]{3,0,2,1:T(1,128)S(1)}, f32[1,7,7,128]{3,0,2,1:T(1,128)S(1)}, u32[]{:S(2)}, u32[]{:S(2)}) %collective-permute-start.43) | collective-permute-done | bytes 25120 | tf_op jit(solution)/shard_map/ppermute | solution.py:23
  282.9 8.0 %collective-permute-start.47 = (f32[9,9,1,128]{3,2,1,0:T(1,128)S(1)}, f32[9,9,1,128]{3,2,1,0:T(1,128)S(1)}, u32[]{:S(2)}, u32[]{:S(2)}) collective-permute-start(f32[9,9,1,128]{3,2,1,0:T(1,128)S(1)} %get-tuple-element.46), channel_id=1, source_target_pairs={{1,0},{2,1},{3,2},{4,3},{5,4},{6,5},{7,6},{8,7},{9,8},{10,9},{11,1... | collective-permute-start | bytes 124424 | tf_op jit(solution)/shard_map/ppermute | solution.py:23
  (265 shorter events, 131.6 us)
Async XLA Ops:
  1.3 14.4 %collective-permute-start = (f32[1,2,2,18,128]{4,3,2,1,0:T(8,128)S(1)}, f32[1,2,2,18,128]{4,3,2,1,0:T(8,128)S(1)}, u32[]{:S(2)}, u32[]{:S(2)}) collective-permute-start(f32[1,2,2,18,128]{4,3,2,1,0:T(8,128)S(1)} %get-tuple-element.115), channel_id=1, source_target_pairs={{0,128},{128,256},{256,384},{384,512},{512,640},{640,0},{1,129},{1... | collective-permute-start | bytes 110600 | tf_op jit(solution)/shard_map/ppermute | solution.py:21
  13.3 9.4 %collective-permute-start.1 = (f32[1,2,2,18,128]{4,3,2,1,0:T(8,128)S(1)}, f32[1,2,2,18,128]{4,3,2,1,0:T(8,128)S(1)}, u32[]{:S(2)}, u32[]{:S(2)}) collective-permute-start(f32[1,2,2,18,128]{4,3,2,1,0:T(8,128)S(1)} %get-tuple-element.116), channel_id=1, source_target_pairs={{128,0},{256,128},{384,256},{512,384},{640,512},{0,640},{129,1},{2... | collective-permute-start | bytes 110600 | tf_op jit(solution)/shard_map/ppermute | solution.py:23
  32.7 13.6 %collective-permute-start.4 = (f32[4,4,1,18,128]{4,3,2,1,0:T(8,128)S(1)}, f32[4,4,1,18,128]{4,3,2,1,0:T(8,128)S(1)}, u32[]{:S(2)}, u32[]{:S(2)}) collective-permute-start(f32[4,4,1,18,128]{4,3,2,1,0:T(8,128)S(1)} %get-tuple-element.43), channel_id=1, source_target_pairs={{0,1},{1,2},{2,3},{3,4},{4,5},{5,6},{6,7},{7,8},{8,9},{9,10},{10,1... | collective-permute-start | bytes 442376 | tf_op jit(solution)/shard_map/ppermute | solution.py:21
  34.6 12.7 %collective-permute-start.5 = (f32[4,4,1,18,128]{4,3,2,1,0:T(8,128)S(1)}, f32[4,4,1,18,128]{4,3,2,1,0:T(8,128)S(1)}, u32[]{:S(2)}, u32[]{:S(2)}) collective-permute-start(f32[4,4,1,18,128]{4,3,2,1,0:T(8,128)S(1)} %get-tuple-element.44), channel_id=1, source_target_pairs={{1,0},{2,1},{3,2},{4,3},{5,4},{6,5},{7,6},{8,7},{9,8},{10,9},{11,1... | collective-permute-start | bytes 442376 | tf_op jit(solution)/shard_map/ppermute | solution.py:23
  51.3 9.2 %collective-permute-start.7 = (f32[1,7,7,128]{3,0,2,1:T(1,128)S(1)}, f32[1,7,7,128]{3,0,2,1:T(1,128)S(1)}, u32[]{:S(2)}, u32[]{:S(2)}) collective-permute-start(f32[1,7,7,128]{3,0,2,1:T(1,128)S(1)} %slice.721), channel_id=1, source_target_pairs={{128,0},{256,128},{384,256},{512,384},{640,512},{0,640},{129,1},{2... | collective-permute-start | bytes 75272 | tf_op jit(solution)/shard_map/ppermute | solution.py:23
  69.1 9.8 %collective-permute-start.10 = (f32[9,9,1,128]{3,2,1,0:T(1,128)S(1)}, f32[9,9,1,128]{3,2,1,0:T(1,128)S(1)}, u32[]{:S(2)}, u32[]{:S(2)}) collective-permute-start(f32[9,9,1,128]{3,2,1,0:T(1,128)S(1)} %get-tuple-element.51), channel_id=1, source_target_pairs={{0,1},{1,2},{2,3},{3,4},{4,5},{5,6},{6,7},{7,8},{8,9},{9,10},{10,1... | collective-permute-start | bytes 124424 | tf_op jit(solution)/shard_map/ppermute | solution.py:21
  84.8 9.6 %collective-permute-start.13 = (f32[1,2,2,18,128]{4,3,2,1,0:T(8,128)S(1)}, f32[1,2,2,18,128]{4,3,2,1,0:T(8,128)S(1)}, u32[]{:S(2)}, u32[]{:S(2)}) collective-permute-start(f32[1,2,2,18,128]{4,3,2,1,0:T(8,128)S(1)} %get-tuple-element.106), channel_id=1, source_target_pairs={{128,0},{256,128},{384,256},{512,384},{640,512},{0,640},{129,1},{2... | collective-permute-start | bytes 110600 | tf_op jit(solution)/shard_map/ppermute | solution.py:23
  105.3 11.9 %collective-permute-start.16 = (f32[4,4,1,18,128]{4,3,2,1,0:T(8,128)S(1)}, f32[4,4,1,18,128]{4,3,2,1,0:T(8,128)S(1)}, u32[]{:S(2)}, u32[]{:S(2)}) collective-permute-start(f32[4,4,1,18,128]{4,3,2,1,0:T(8,128)S(1)} %get-tuple-element.39), channel_id=1, source_target_pairs={{0,1},{1,2},{2,3},{3,4},{4,5},{5,6},{6,7},{7,8},{8,9},{9,10},{10,1... | collective-permute-start | bytes 442376 | tf_op jit(solution)/shard_map/ppermute | solution.py:21
  107.2 11.8 %collective-permute-start.17 = (f32[4,4,1,18,128]{4,3,2,1,0:T(8,128)S(1)}, f32[4,4,1,18,128]{4,3,2,1,0:T(8,128)S(1)}, u32[]{:S(2)}, u32[]{:S(2)}) collective-permute-start(f32[4,4,1,18,128]{4,3,2,1,0:T(8,128)S(1)} %get-tuple-element.40), channel_id=1, source_target_pairs={{1,0},{2,1},{3,2},{4,3},{5,4},{6,5},{7,6},{8,7},{9,8},{10,9},{11,1... | collective-permute-start | bytes 442376 | tf_op jit(solution)/shard_map/ppermute | solution.py:23
  122.4 9.1 %collective-permute-start.19 = (f32[1,7,7,128]{3,0,2,1:T(1,128)S(1)}, f32[1,7,7,128]{3,0,2,1:T(1,128)S(1)}, u32[]{:S(2)}, u32[]{:S(2)}) collective-permute-start(f32[1,7,7,128]{3,0,2,1:T(1,128)S(1)} %slice.778), channel_id=1, source_target_pairs={{128,0},{256,128},{384,256},{512,384},{640,512},{0,640},{129,1},{2... | collective-permute-start | bytes 75272 | tf_op jit(solution)/shard_map/ppermute | solution.py:23
  139.9 10.0 %collective-permute-start.22 = (f32[9,9,1,128]{3,2,1,0:T(1,128)S(1)}, f32[9,9,1,128]{3,2,1,0:T(1,128)S(1)}, u32[]{:S(2)}, u32[]{:S(2)}) collective-permute-start(f32[9,9,1,128]{3,2,1,0:T(1,128)S(1)} %get-tuple-element.49), channel_id=1, source_target_pairs={{0,1},{1,2},{2,3},{3,4},{4,5},{5,6},{6,7},{7,8},{8,9},{9,10},{10,1... | collective-permute-start | bytes 124424 | tf_op jit(solution)/shard_map/ppermute | solution.py:21
  141.8 9.1 %collective-permute-start.23 = (f32[9,9,1,128]{3,2,1,0:T(1,128)S(1)}, f32[9,9,1,128]{3,2,1,0:T(1,128)S(1)}, u32[]{:S(2)}, u32[]{:S(2)}) collective-permute-start(f32[9,9,1,128]{3,2,1,0:T(1,128)S(1)} %get-tuple-element.50), channel_id=1, source_target_pairs={{1,0},{2,1},{3,2},{4,3},{5,4},{6,5},{7,6},{8,7},{9,8},{10,9},{11,1... | collective-permute-start | bytes 124424 | tf_op jit(solution)/shard_map/ppermute | solution.py:23
  156.0 9.3 %collective-permute-start.25 = (f32[1,2,2,18,128]{4,3,2,1,0:T(8,128)S(1)}, f32[1,2,2,18,128]{4,3,2,1,0:T(8,128)S(1)}, u32[]{:S(2)}, u32[]{:S(2)}) collective-permute-start(f32[1,2,2,18,128]{4,3,2,1,0:T(8,128)S(1)} %get-tuple-element.96), channel_id=1, source_target_pairs={{128,0},{256,128},{384,256},{512,384},{640,512},{0,640},{129,1},{2... | collective-permute-start | bytes 110600 | tf_op jit(solution)/shard_map/ppermute | solution.py:23
  174.5 11.7 %collective-permute-start.28 = (f32[4,4,1,18,128]{4,3,2,1,0:T(8,128)S(1)}, f32[4,4,1,18,128]{4,3,2,1,0:T(8,128)S(1)}, u32[]{:S(2)}, u32[]{:S(2)}) collective-permute-start(f32[4,4,1,18,128]{4,3,2,1,0:T(8,128)S(1)} %get-tuple-element.35), channel_id=1, source_target_pairs={{0,1},{1,2},{2,3},{3,4},{4,5},{5,6},{6,7},{7,8},{8,9},{9,10},{10,1... | collective-permute-start | bytes 442376 | tf_op jit(solution)/shard_map/ppermute | solution.py:21
  176.5 10.7 %collective-permute-start.29 = (f32[4,4,1,18,128]{4,3,2,1,0:T(8,128)S(1)}, f32[4,4,1,18,128]{4,3,2,1,0:T(8,128)S(1)}, u32[]{:S(2)}, u32[]{:S(2)}) collective-permute-start(f32[4,4,1,18,128]{4,3,2,1,0:T(8,128)S(1)} %get-tuple-element.36), channel_id=1, source_target_pairs={{1,0},{2,1},{3,2},{4,3},{5,4},{6,5},{7,6},{8,7},{9,8},{10,9},{11,1... | collective-permute-start | bytes 442376 | tf_op jit(solution)/shard_map/ppermute | solution.py:23
  191.4 9.1 %collective-permute-start.31 = (f32[1,7,7,128]{3,0,2,1:T(1,128)S(1)}, f32[1,7,7,128]{3,0,2,1:T(1,128)S(1)}, u32[]{:S(2)}, u32[]{:S(2)}) collective-permute-start(f32[1,7,7,128]{3,0,2,1:T(1,128)S(1)} %slice.835), channel_id=1, source_target_pairs={{128,0},{256,128},{384,256},{512,384},{640,512},{0,640},{129,1},{2... | collective-permute-start | bytes 75272 | tf_op jit(solution)/shard_map/ppermute | solution.py:23
  209.1 10.2 %collective-permute-start.34 = (f32[9,9,1,128]{3,2,1,0:T(1,128)S(1)}, f32[9,9,1,128]{3,2,1,0:T(1,128)S(1)}, u32[]{:S(2)}, u32[]{:S(2)}) collective-permute-start(f32[9,9,1,128]{3,2,1,0:T(1,128)S(1)} %get-tuple-element.47), channel_id=1, source_target_pairs={{0,1},{1,2},{2,3},{3,4},{4,5},{5,6},{6,7},{7,8},{8,9},{9,10},{10,1... | collective-permute-start | bytes 124424 | tf_op jit(solution)/shard_map/ppermute | solution.py:21
  211.1 9.3 %collective-permute-start.35 = (f32[9,9,1,128]{3,2,1,0:T(1,128)S(1)}, f32[9,9,1,128]{3,2,1,0:T(1,128)S(1)}, u32[]{:S(2)}, u32[]{:S(2)}) collective-permute-start(f32[9,9,1,128]{3,2,1,0:T(1,128)S(1)} %get-tuple-element.48), channel_id=1, source_target_pairs={{1,0},{2,1},{3,2},{4,3},{5,4},{6,5},{7,6},{8,7},{9,8},{10,9},{11,1... | collective-permute-start | bytes 124424 | tf_op jit(solution)/shard_map/ppermute | solution.py:23
  226.3 9.3 %collective-permute-start.37 = (f32[1,2,2,18,128]{4,3,2,1,0:T(8,128)S(1)}, f32[1,2,2,18,128]{4,3,2,1,0:T(8,128)S(1)}, u32[]{:S(2)}, u32[]{:S(2)}) collective-permute-start(f32[1,2,2,18,128]{4,3,2,1,0:T(8,128)S(1)} %get-tuple-element.86), channel_id=1, source_target_pairs={{128,0},{256,128},{384,256},{512,384},{640,512},{0,640},{129,1},{2... | collective-permute-start | bytes 110600 | tf_op jit(solution)/shard_map/ppermute | solution.py:23
  246.1 12.7 %collective-permute-start.40 = (f32[4,4,1,18,128]{4,3,2,1,0:T(8,128)S(1)}, f32[4,4,1,18,128]{4,3,2,1,0:T(8,128)S(1)}, u32[]{:S(2)}, u32[]{:S(2)}) collective-permute-start(f32[4,4,1,18,128]{4,3,2,1,0:T(8,128)S(1)} %get-tuple-element.31), channel_id=1, source_target_pairs={{0,1},{1,2},{2,3},{3,4},{4,5},{5,6},{6,7},{7,8},{8,9},{9,10},{10,1... | collective-permute-start | bytes 442376 | tf_op jit(solution)/shard_map/ppermute | solution.py:21
  248.0 12.4 %collective-permute-start.41 = (f32[4,4,1,18,128]{4,3,2,1,0:T(8,128)S(1)}, f32[4,4,1,18,128]{4,3,2,1,0:T(8,128)S(1)}, u32[]{:S(2)}, u32[]{:S(2)}) collective-permute-start(f32[4,4,1,18,128]{4,3,2,1,0:T(8,128)S(1)} %get-tuple-element.32), channel_id=1, source_target_pairs={{1,0},{2,1},{3,2},{4,3},{5,4},{6,5},{7,6},{8,7},{9,8},{10,9},{11,1... | collective-permute-start | bytes 442376 | tf_op jit(solution)/shard_map/ppermute | solution.py:23
  263.6 9.1 %collective-permute-start.43 = (f32[1,7,7,128]{3,0,2,1:T(1,128)S(1)}, f32[1,7,7,128]{3,0,2,1:T(1,128)S(1)}, u32[]{:S(2)}, u32[]{:S(2)}) collective-permute-start(f32[1,7,7,128]{3,0,2,1:T(1,128)S(1)} %slice.892), channel_id=1, source_target_pairs={{128,0},{256,128},{384,256},{512,384},{640,512},{0,640},{129,1},{2... | collective-permute-start | bytes 75272 | tf_op jit(solution)/shard_map/ppermute | solution.py:23
  280.9 10.0 %collective-permute-start.46 = (f32[9,9,1,128]{3,2,1,0:T(1,128)S(1)}, f32[9,9,1,128]{3,2,1,0:T(1,128)S(1)}, u32[]{:S(2)}, u32[]{:S(2)}) collective-permute-start(f32[9,9,1,128]{3,2,1,0:T(1,128)S(1)} %get-tuple-element.45), channel_id=1, source_target_pairs={{0,1},{1,2},{2,3},{3,4},{4,5},{5,6},{6,7},{7,8},{8,9},{9,10},{10,1... | collective-permute-start | bytes 124424 | tf_op jit(solution)/shard_map/ppermute | solution.py:21
  282.9 9.1 %collective-permute-start.47 = (f32[9,9,1,128]{3,2,1,0:T(1,128)S(1)}, f32[9,9,1,128]{3,2,1,0:T(1,128)S(1)}, u32[]{:S(2)}, u32[]{:S(2)}) collective-permute-start(f32[9,9,1,128]{3,2,1,0:T(1,128)S(1)} %get-tuple-element.46), channel_id=1, source_target_pairs={{1,0},{2,1},{3,2},{4,3},{5,4},{6,5},{7,6},{8,7},{9,8},{10,9},{11,1... | collective-permute-start | bytes 124424 | tf_op jit(solution)/shard_map/ppermute | solution.py:23
  (29 other events, 221.0 us)
where the time goes:
time: 297 us; the launch traced here: 293 us
  starting transfers between devices  184 us (62%)
  waiting for transfers between devices  96.3 us (32%)
  matrix products  4.2 us (1%)
  other arithmetic  3.58 us (1%)
  local copies, waits for them, and re-layouts  3.05 us (1%)
    ppermute x24, starting transfers between devices, with_halo(): lax.ppermute(head, axis, [((i + 1) % count, i) for i in range(count)])  106 us
    ppermute x24, waiting for transfers between devices, with_halo(): lax.ppermute(head, axis, [((i + 1) % count, i) for i in range(count)])  82.1 us
    ppermute x24, starting transfers between devices, with_halo(): lax.ppermute(tail, axis, [(i, (i + 1) % count) for i in range(count)])  78 us
    ppermute x24, waiting for transfers between devices, with_halo(): lax.ppermute(tail, axis, [(i, (i + 1) % count) for i in range(count)])  14.2 us
  transfers between devices with their start and end apart: 48, of which 32 were waited for; matrix products, arithmetic and copies ran while one was open for 0% of the time, Pallas kernels for 0%

commit v1 on v0

v1 whole, which is shorter than its diff:
```python
import jax
import jax.numpy as jnp
from jax import lax
from jax.sharding import PartitionSpec as P

PDEG = 6
ORDER = 4

CENTER = 0.1
HALF = 2.0

AXES = ("gx", "gy", "gz")
FIRST = (1, 0, 0)
SECOND = (0, 1, 1)
RELATIVE = [(x, y, z) for x in range(2) for y in range(2) for z in range(2)]


def bricks(sizes, offsets):
    groups = []
    for i in range(0, sizes[0], 2):
        for j in range(0, sizes[1], 2):
            for k in range(0, sizes[2], 2):
                members = []
                for a, b, c in RELATIVE:
                    x = (i + a + offsets[0]) % sizes[0]
                    y = (j + b + offsets[1]) % sizes[1]
                    z = (k + c + offsets[2]) % sizes[2]
                    members.append((x * sizes[1] + y) * sizes[2] + z)
                groups.append(members)
    return groups


def brick_exchange(chunks, offsets, rows):
    sizes = [lax.axis_size(axis) for axis in AXES]
    bits = [(lax.axis_index(axis) + sizes[d] - offsets[d]) % 2 for d, axis in enumerate(AXES)]
    me = 4 * bits[0] + 2 * bits[1] + bits[2]
    stacked = jnp.stack([jnp.pad(c, ((0, rows - c.shape[0]), (0, 0))) for c in chunks])
    ordered = jnp.stack([lax.dynamic_index_in_dim(stacked, me ^ t, 0, keepdims=False) for t in range(8)])
    arrived = lax.all_to_all(ordered, AXES, 0, 0, axis_index_groups=bricks(sizes, offsets))
    return [
        lax.dynamic_index_in_dim(arrived, me ^ r, 0, keepdims=False)[: chunks[r].shape[0]] for r in range(8)
    ]


def side_slice(values, relative, index):
    for d in range(3):
        if relative[d]:
            values = lax.slice_in_dim(values, index, index + 1, axis=d)
    return values


def side_rows(values, relative, index):
    part = side_slice(values, relative, index)
    return part.reshape(-1, values.shape[-1])


def side_place(rows, relative, index, shape):
    part_shape = tuple(1 if d < 3 and relative[d] else n for d, n in enumerate(shape))
    part = rows.reshape(part_shape)
    pads = [
        (index, shape[d] - 1 - index, 0) if d < 3 and relative[d] else (0, 0, 0) for d in range(len(shape))
    ]
    return lax.pad(part, jnp.zeros((), rows.dtype), pads)


def brick_sum(values, offsets, index, rows):
    chunks = [side_rows(values, r, index) for r in RELATIVE]
    chunks[0] = jnp.zeros((8, values.shape[-1]), values.dtype)
    arrived = brick_exchange(chunks, offsets, rows)
    total = values
    for r, part in zip(RELATIVE[1:], arrived[1:]):
        total = total + side_place(part, r, index, values.shape)
    return total


def mirrored(values, flips):
    for d in range(3):
        values = jnp.where(flips[d], jnp.flip(values, d), values)
    return values


def exact_dot(a, b, dims):
    return lax.dot_general(a, b, (dims, ((), ())), preferred_element_type=jnp.float32).astype(a.dtype)


def local(wavefunctions, cell_hamiltonian, projectors, atom_species, coupling):
    node_count = cell_hamiltonian.shape[3]
    side = PDEG + 1
    width = wavefunctions.shape[3]
    nproj = projectors.shape[4]
    sizes = [lax.axis_size(axis) for axis in AXES]
    flips = [
        ((lax.axis_index(axis) + sizes[d] - FIRST[d]) % 2) == 1 for d, axis in enumerate(AXES)
    ]
    node = lax.broadcasted_iota(jnp.int32, (node_count, node_count), 0)
    other = lax.broadcasted_iota(jnp.int32, (node_count, node_count), 1)
    place = [node // (side * side), (node // side) % side, node % side]
    place = [jnp.where(f, side - 1 - p, p) for f, p in zip(flips, place)]
    mirror = (other == (place[0] * side + place[1]) * side + place[2]).astype(jnp.bfloat16)

    hamiltonian = cell_hamiltonian.reshape(node_count, node_count)
    hamiltonian = exact_dot(exact_dot(mirror, hamiltonian, ((1,), (0,))), mirror, ((1,), (0,)))
    betas = mirrored(projectors.reshape(2, 2, 2, nproj, node_count), flips).reshape(8 * nproj, node_count)
    betas = exact_dot(betas, mirror, ((1,), (0,)))
    start = exact_dot(mirror, wavefunctions.reshape(node_count, width), ((1,), (0,)))

    kinds = jnp.arange(1, coupling.shape[0] + 1, dtype=jnp.int32)
    species_mask = (mirrored(atom_species, flips)[..., None] == kinds).astype(jnp.float32)
    vertex_coupling = jnp.einsum(
        "xyzs,spq->xyzpq", species_mask, coupling, precision=lax.Precision.HIGHEST
    )

    current = start
    previous = start
    for step in range(ORDER):
        partial_value = jnp.dot(betas, current, preferred_element_type=jnp.float32)
        partial_value = partial_value.reshape(2, 2, 2, nproj, width)
        correlations = brick_sum(partial_value, FIRST, 1, 4 * nproj)
        correlations = brick_sum(correlations, SECOND, 0, 4 * nproj)
        coefficients = jnp.einsum(
            "xyzpq,xyzqw->xyzpw", vertex_coupling, correlations, precision=lax.Precision.HIGHEST
        ).astype(jnp.bfloat16)
        terms = jnp.dot(hamiltonian, current, preferred_element_type=jnp.float32)
        terms = terms + lax.dot_general(
            betas,
            coefficients.reshape(8 * nproj, width),
            (((0,), (0,)), ((), ())),
            preferred_element_type=jnp.float32,
        )
        terms = terms.reshape(side, side, side, width)
        applied = brick_sum(terms, SECOND, 0, 56)
        applied = brick_sum(applied, FIRST, side - 1, 56).reshape(node_count, width)
        current_wide = current.astype(jnp.float32)
        if step == 0:
            updated = (applied - CENTER * current_wide) / HALF
        else:
            updated = 2.0 * (applied - CENTER * current_wide) / HALF - previous.astype(jnp.float32)
        previous = current
        current = updated.astype(jnp.bfloat16)
    return exact_dot(mirror, current, ((1,), (0,))).reshape(wavefunctions.shape)


def solution(mesh):
    placed = (
        P("gx", "gy", "gz", None),
        P("gx", "gy", "gz", None, None),
        P("gx", "gy", "gz", None, None, None),
        P("gx", "gy", "gz"),
        P(),
    )
    return jax.shard_map(
        local, mesh=mesh, in_specs=placed, out_specs=P("gx", "gy", "gz", None), check_vma=False
    )
```

time: 297 us -> 328 us (1.10)
  blocking collectives: 0 us -> 159 us
  starting transfers between devices: 184 us -> 54.3 us
  waiting for transfers between devices: 96.3 us -> 19.8 us
  local copies, waits for them, and re-layouts: 3.05 us -> 78.1 us
  matrix products: 4.2 us -> 7.87 us
    ppermute x48 -> x0, starting transfers between devices: 184 us -> none  [the longest x24 106 us: with_halo(): lax.ppermute(head, axis, [((i + 1) % count, i) for i in range(count)])]
    all_to_all x0 -> x11, blocking collectives: none -> 159 us  [brick_exchange(): lax.all_to_all(ordered, AXES, 0, 0, axis_index_groups=bricks(sizes, offse...]
    ppermute x48 -> x0, waiting for transfers between devices: 96.3 us -> none  [the longest x24 82.1 us: with_halo(): lax.ppermute(head, axis, [((i + 1) % count, i) for i in range(count)])]
    all_to_all x0 -> x5, starting transfers between devices: none -> 54.3 us  [brick_exchange(): lax.all_to_all(ordered, AXES, 0, 0, axis_index_groups=bricks(sizes, offse...]
    unnamed x46 -> x343, local copies, waits for them, and re-layouts: 0.84 us -> 50.4 us
    all_to_all x0 -> x5, waiting for transfers between devices: none -> 19.8 us  [brick_exchange(): lax.all_to_all(ordered, AXES, 0, 0, axis_index_groups=bricks(sizes, offse...]
    slice x40 -> x140, local copies, waits for them, and re-layouts: 0.73 us -> 17.4 us  [the longest x120 16.6 us: side_slice(): values = lax.slice_in_dim(values, index, index + 1, axis=d)]
    reshape x0 -> x181, local copies, waits for them, and re-layouts: none -> 6.12 us  [the longest x93 4.82 us: side_place(): part = rows.reshape(part_shape)]
  transfers between devices with their start and end apart: 48 -> 5, of which waited for: 32 -> 5; matrix products, arithmetic and copies ran while one was open for 0% -> 2% of each run, Pallas kernels for 0% -> 0%
where the time goes in v1:
time: 328 us; the launch traced here: 325 us
  blocking collectives  159 us (48%)
  local copies, waits for them, and re-layouts  78.1 us (24%)
  starting transfers between devices  54.3 us (17%)
  waiting for transfers between devices  19.8 us (6%)
  matrix products  7.87 us (2%)
  between operations  4.49 us (1%)
    all_to_all x11, blocking collectives, brick_exchange(): lax.all_to_all(ordered, AXES, 0, 0, axis_index_groups=bricks(sizes, offse...  159 us
    all_to_all x5, starting transfers between devices, brick_exchange(): lax.all_to_all(ordered, AXES, 0, 0, axis_index_groups=bricks(sizes, offse...  54.3 us
    unnamed x343, local copies, waits for them, and re-layouts  50.4 us
    all_to_all x5, waiting for transfers between devices, brick_exchange(): lax.all_to_all(ordered, AXES, 0, 0, axis_index_groups=bricks(sizes, offse...  19.8 us
    slice x120, local copies, waits for them, and re-layouts, side_slice(): values = lax.slice_in_dim(values, index, index + 1, axis=d)  16.6 us
  transfers between devices with their start and end apart: 5, of which 5 were waited for; matrix products, arithmetic and copies ran while one was open for 2% of the time, Pallas kernels for 0%

profile of v1, /device:TPU:1, one launch (start us, length us, event | category | flops | bytes accessed | tf_op | source)
XLA Modules:
  0.0 325.0 jit_solution(16247078151611825804)
XLA Ops:
  12.5 13.3 %all-to-all-start = ((f32[8,72,128]{2,1,0:T(8,128)}), f32[8,72,128]{2,1,0:T(8,128)S(1)}, u32[]{:S(2)}, u32[]{:S(2)}) async-start(f32[8,72,128]{2,1,0:T(8,128)} %constant_dynamic-update-slice_fusion.8), calls=%async_computation | async-start | bytes 589824 | tf_op jit(solution)/shard_map/all_to_all | solution.py:39
  30.9 5.3 %all-to-all-done = f32[8,72,128]{2,1,0:T(8,128)S(1)} async-done(((f32[8,72,128]{2,1,0:T(8,128)}), f32[8,72,128]{2,1,0:T(8,128)S(1)}, u32[]{:S(2)}, u32[]{:S(2)}) %all-to-all-start) | async-done | bytes 294944 | tf_op jit(solution)/shard_map/all_to_all | solution.py:39
  44.5 13.9 %all-to-all-start.1 = ((f32[8,72,128]{2,1,0:T(8,128)}), f32[8,72,128]{2,1,0:T(8,128)S(1)}, u32[]{:S(2)}, u32[]{:S(2)}) async-start(f32[8,72,128]{2,1,0:T(8,128)} %constant_dynamic-update-slice_fusion.24), calls=%async_computation.1 | async-start | bytes 589824 | tf_op jit(solution)/shard_map/all_to_all | solution.py:39
  60.1 2.5 all-to-all-done.1
  63.3 1.4 reshape.1146
  64.7 1.3 reshape.1147
  66.0 1.3 reshape.1148
  70.6 13.7 %all_to_all.80 = f32[8,56,128]{2,1,0:T(8,128)S(1)} all-to-all(f32[8,56,128]{2,1,0:T(8,128)S(1)} %constant_dynamic-update-slice_fusion.40), channel_id=1, replica_groups={{17,18,33,34,145,146,161,162},{19,20,35,36,147,148,163,164},{21,22,37,3..., dimensions={0} | all-to-all | bytes 458752 | tf_op jit(solution)/shard_map/all_to_all | solution.py:39
  85.8 16.3 %all_to_all.81 = f32[8,56,128]{2,1,0:T(8,128)S(1)} all-to-all(f32[8,56,128]{2,1,0:T(8,128)S(1)} %constant_dynamic-update-slice_fusion.56), channel_id=1, replica_groups={{128,129,144,145,256,257,272,273},{130,131,146,147,258,259,274,275},{13..., dimensions={0} | all-to-all | bytes 458752 | tf_op jit(solution)/shard_map/all_to_all | solution.py:39
  106.6 16.3 %all_to_all.82 = f32[8,72,128]{2,1,0:T(8,128)S(1)} all-to-all(f32[8,72,128]{2,1,0:T(8,128)S(1)} %constant_dynamic-update-slice_fusion.72), channel_id=1, replica_groups={{128,129,144,145,256,257,272,273},{130,131,146,147,258,259,274,275},{13..., dimensions={0} | all-to-all | bytes 589824 | tf_op jit(solution)/shard_map/all_to_all | solution.py:39
  131.2 9.0 %all-to-all-start.5 = ((f32[8,72,128]{2,1,0:T(8,128)}), f32[8,72,128]{2,1,0:T(8,128)S(1)}, u32[]{:S(2)}, u32[]{:S(2)}) async-start(f32[8,72,128]{2,1,0:T(8,128)} %constant_dynamic-update-slice_fusion.88), calls=%async_computation.5 | async-start | bytes 589824 | tf_op jit(solution)/shard_map/all_to_all | solution.py:39
  140.5 4.0 %all-to-all-done.5 = f32[8,72,128]{2,1,0:T(8,128)S(1)} async-done(((f32[8,72,128]{2,1,0:T(8,128)}), f32[8,72,128]{2,1,0:T(8,128)S(1)}, u32[]{:S(2)}, u32[]{:S(2)}) %all-to-all-start.5) | async-done | bytes 294944 | tf_op jit(solution)/shard_map/all_to_all | solution.py:39
  147.4 13.8 %all_to_all.83 = f32[8,56,128]{2,1,0:T(8,128)S(1)} all-to-all(f32[8,56,128]{2,1,0:T(8,128)S(1)} %constant_dynamic-update-slice_fusion.104), channel_id=1, replica_groups={{17,18,33,34,145,146,161,162},{19,20,35,36,147,148,163,164},{21,22,37,3..., dimensions={0} | all-to-all | bytes 458752 | tf_op jit(solution)/shard_map/all_to_all | solution.py:39
  162.5 13.5 %all_to_all.84 = f32[8,56,128]{2,1,0:T(8,128)S(1)} all-to-all(f32[8,56,128]{2,1,0:T(8,128)S(1)} %constant_dynamic-update-slice_fusion.120), channel_id=1, replica_groups={{128,129,144,145,256,257,272,273},{130,131,146,147,258,259,274,275},{13..., dimensions={0} | all-to-all | bytes 458752 | tf_op jit(solution)/shard_map/all_to_all | solution.py:39
  180.6 14.7 %all_to_all.85 = f32[8,72,128]{2,1,0:T(8,128)S(1)} all-to-all(f32[8,72,128]{2,1,0:T(8,128)S(1)} %constant_dynamic-update-slice_fusion.136), channel_id=1, replica_groups={{128,129,144,145,256,257,272,273},{130,131,146,147,258,259,274,275},{13..., dimensions={0} | all-to-all | bytes 589824 | tf_op jit(solution)/shard_map/all_to_all | solution.py:39
  203.6 9.0 %all-to-all-start.9 = ((f32[8,72,128]{2,1,0:T(8,128)}), f32[8,72,128]{2,1,0:T(8,128)S(1)}, u32[]{:S(2)}, u32[]{:S(2)}) async-start(f32[8,72,128]{2,1,0:T(8,128)} %constant_dynamic-update-slice_fusion.152), calls=%async_computation.9 | async-start | bytes 589824 | tf_op jit(solution)/shard_map/all_to_all | solution.py:39
  212.9 4.1 %all-to-all-done.9 = f32[8,72,128]{2,1,0:T(8,128)S(1)} async-done(((f32[8,72,128]{2,1,0:T(8,128)}), f32[8,72,128]{2,1,0:T(8,128)S(1)}, u32[]{:S(2)}, u32[]{:S(2)}) %all-to-all-start.9) | async-done | bytes 294944 | tf_op jit(solution)/shard_map/all_to_all | solution.py:39
  219.8 13.6 %all_to_all.86 = f32[8,56,128]{2,1,0:T(8,128)S(1)} all-to-all(f32[8,56,128]{2,1,0:T(8,128)S(1)} %constant_dynamic-update-slice_fusion.168), channel_id=1, replica_groups={{17,18,33,34,145,146,161,162},{19,20,35,36,147,148,163,164},{21,22,37,3..., dimensions={0} | all-to-all | bytes 458752 | tf_op jit(solution)/shard_map/all_to_all | solution.py:39
  234.9 15.5 %all_to_all.87 = f32[8,56,128]{2,1,0:T(8,128)S(1)} all-to-all(f32[8,56,128]{2,1,0:T(8,128)S(1)} %constant_dynamic-update-slice_fusion.184), channel_id=1, replica_groups={{128,129,144,145,256,257,272,273},{130,131,146,147,258,259,274,275},{13..., dimensions={0} | all-to-all | bytes 458752 | tf_op jit(solution)/shard_map/all_to_all | solution.py:39
  255.0 14.1 %all_to_all.88 = f32[8,72,128]{2,1,0:T(8,128)S(1)} all-to-all(f32[8,72,128]{2,1,0:T(8,128)S(1)} %constant_dynamic-update-slice_fusion.200), channel_id=1, replica_groups={{128,129,144,145,256,257,272,273},{130,131,146,147,258,259,274,275},{13..., dimensions={0} | all-to-all | bytes 589824 | tf_op jit(solution)/shard_map/all_to_all | solution.py:39
  277.5 9.0 %all-to-all-start.13 = ((f32[8,72,128]{2,1,0:T(8,128)}), f32[8,72,128]{2,1,0:T(8,128)S(1)}, u32[]{:S(2)}, u32[]{:S(2)}) async-start(f32[8,72,128]{2,1,0:T(8,128)} %constant_dynamic-update-slice_fusion.216), calls=%async_computation.13 | async-start | bytes 589824 | tf_op jit(solution)/shard_map/all_to_all | solution.py:39
  286.8 4.0 %all-to-all-done.13 = f32[8,72,128]{2,1,0:T(8,128)S(1)} async-done(((f32[8,72,128]{2,1,0:T(8,128)}), f32[8,72,128]{2,1,0:T(8,128)S(1)}, u32[]{:S(2)}, u32[]{:S(2)}) %all-to-all-start.13) | async-done | bytes 294944 | tf_op jit(solution)/shard_map/all_to_all | solution.py:39
  293.6 13.8 %all_to_all.89 = f32[8,56,128]{2,1,0:T(8,128)S(1)} all-to-all(f32[8,56,128]{2,1,0:T(8,128)S(1)} %constant_dynamic-update-slice_fusion.232), channel_id=1, replica_groups={{17,18,33,34,145,146,161,162},{19,20,35,36,147,148,163,164},{21,22,37,3..., dimensions={0} | all-to-all | bytes 458752 | tf_op jit(solution)/shard_map/all_to_all | solution.py:39
  308.8 14.0 %all_to_all.90 = f32[8,56,128]{2,1,0:T(8,128)S(1)} all-to-all(f32[8,56,128]{2,1,0:T(8,128)S(1)} %constant_dynamic-update-slice_fusion.248), channel_id=1, replica_groups={{128,129,144,145,256,257,272,273},{130,131,146,147,258,259,274,275},{13..., dimensions={0} | all-to-all | bytes 458752 | tf_op jit(solution)/shard_map/all_to_all | solution.py:39
  (777 shorter events, 83.1 us)
Async XLA Ops:
  0.0 58.7 %copy-start = (bf16[1,1,1,343,343]{4,3,2,1,0:T(8,128)(2,1)S(1)}, bf16[1,1,1,343,343]{4,3,2,1,0:T(8,128)(2,1)}, u32[]{:S(2)}) copy-start(bf16[1,1,1,343,343]{4,3,2,1,0:T(8,128)(2,1)} %param.6) | copy-start | bytes 705898
  0.0 58.6 %copy-start.33 = (s32[343]{0:T(512)}, s32[343]{0:T(512)S(1)}, u32[]{:S(2)}) copy-start(s32[343]{0:T(512)S(1)} %get-tuple-element.106) | copy-start | bytes 4120
  0.0 58.6 %copy-start.35 = (s32[343]{0:T(512)}, s32[343]{0:T(512)S(1)}, u32[]{:S(2)}) copy-start(s32[343]{0:T(512)S(1)} %get-tuple-element.107) | copy-start | bytes 4120
  0.1 58.6 %copy-start.37 = (s32[343]{0:T(512)}, s32[343]{0:T(512)S(1)}, u32[]{:S(2)}) copy-start(s32[343]{0:T(512)S(1)} %get-tuple-element.108) | copy-start | bytes 4120
  0.1 58.6 %copy-start.40 = (pred[343]{0:T(512)(128)(4,1)}, pred[343]{0:T(512)(128)(4,1)S(1)}, u32[]{:S(2)}) copy-start(pred[343]{0:T(512)(128)(4,1)S(1)} %get-tuple-element.101) | copy-start | bytes 1033
  0.1 58.6 %copy-start.42 = (pred[343]{0:T(512)(128)(4,1)}, pred[343]{0:T(512)(128)(4,1)S(1)}, u32[]{:S(2)}) copy-start(pred[343]{0:T(512)(128)(4,1)S(1)} %get-tuple-element.102) | copy-start | bytes 1033
  0.1 58.6 %copy-start.44 = (pred[343]{0:T(512)(128)(4,1)}, pred[343]{0:T(512)(128)(4,1)S(1)}, u32[]{:S(2)}) copy-start(pred[343]{0:T(512)(128)(4,1)S(1)} %fusion.134) | copy-start | bytes 1033
  0.3 0.9 copy-start.28
  1.4 0.9 copy-start.29
  12.5 23.6 %all-to-all-start = ((f32[8,72,128]{2,1,0:T(8,128)}), f32[8,72,128]{2,1,0:T(8,128)S(1)}, u32[]{:S(2)}, u32[]{:S(2)}) async-start(f32[8,72,128]{2,1,0:T(8,128)} %constant_dynamic-update-slice_fusion.8), calls=%async_computation | async-start | bytes 589824 | tf_op jit(solution)/shard_map/all_to_all | solution.py:39
  44.5 13.9 %copy-start.39 = (f32[2,18,18]{2,0,1:T(2,128)S(1)}, f32[2,18,18]{2,0,1:T(2,128)}, u32[]{:S(2)}) copy-start(f32[2,18,18]{2,0,1:T(2,128)} %param.9) | copy-start | bytes 7780
  44.5 18.1 %all-to-all-start.1 = ((f32[8,72,128]{2,1,0:T(8,128)}), f32[8,72,128]{2,1,0:T(8,128)S(1)}, u32[]{:S(2)}, u32[]{:S(2)}) async-start(f32[8,72,128]{2,1,0:T(8,128)} %constant_dynamic-update-slice_fusion.24), calls=%async_computation.1 | async-start | bytes 589824 | tf_op jit(solution)/shard_map/all_to_all | solution.py:39
  63.3 4.1 %copy-start.2 = (f32[2,2,2,18,128]{4,3,2,1,0:T(8,128)S(1)}, f32[2,2,2,18,128]{4,3,2,1,0:T(8,128)}, u32[]{:S(2)}) copy-start(f32[2,2,2,18,128]{4,3,2,1,0:T(8,128)} %copy-done.1) | copy-start | bytes 221188
  84.5 0.9 copy-start.23
  131.2 13.3 %all-to-all-start.5 = ((f32[8,72,128]{2,1,0:T(8,128)}), f32[8,72,128]{2,1,0:T(8,128)S(1)}, u32[]{:S(2)}, u32[]{:S(2)}) async-start(f32[8,72,128]{2,1,0:T(8,128)} %constant_dynamic-update-slice_fusion.88), calls=%async_computation.5 | async-start | bytes 589824 | tf_op jit(solution)/shard_map/all_to_all | solution.py:39
  146.1 0.9 copy-start.22
  161.3 0.9 copy-start.21
  203.6 13.4 %all-to-all-start.9 = ((f32[8,72,128]{2,1,0:T(8,128)}), f32[8,72,128]{2,1,0:T(8,128)S(1)}, u32[]{:S(2)}, u32[]{:S(2)}) async-start(f32[8,72,128]{2,1,0:T(8,128)} %constant_dynamic-update-slice_fusion.152), calls=%async_computation.9 | async-start | bytes 589824 | tf_op jit(solution)/shard_map/all_to_all | solution.py:39
  217.1 0.9 copy-start.8
  218.6 0.9 copy-start.20
  233.7 0.9 copy-start.19
  277.5 13.2 %all-to-all-start.13 = ((f32[8,72,128]{2,1,0:T(8,128)}), f32[8,72,128]{2,1,0:T(8,128)S(1)}, u32[]{:S(2)}, u32[]{:S(2)}) async-start(f32[8,72,128]{2,1,0:T(8,128)} %constant_dynamic-update-slice_fusion.216), calls=%async_computation.13 | async-start | bytes 589824 | tf_op jit(solution)/shard_map/all_to_all | solution.py:39
  292.3 0.9 copy-start.18
  307.5 0.9 copy-start.17
  (51 other events, 37.9 us)

commit v2 on v1

v2 whole, which is shorter than its diff:
```python
import functools

import jax
import jax.numpy as jnp
import numpy as np
from jax import lax
from jax.experimental import pallas as pl
from jax.experimental.pallas import tpu as pltpu
from jax.sharding import PartitionSpec as P

PDEG = 6
ORDER = 4

CENTER = 0.1
HALF = 2.0

INTERPRET = False

SIDE = PDEG + 1
ROW = 8
NODES = SIDE * SIDE * ROW
NP = 18
CP = 8 * NP
W = 128
CHUNK = 128
FACE = 72
EDGE = 112
LAST = 127

AXES = ("gx", "gy", "gz")
OFFSETS = {1: (1, 0, 0), 0: (0, 1, 1)}
RELATIVE = [(x, y, z) for x in range(2) for y in range(2) for z in range(2)]


def bricks(sizes, offsets):
    groups = []
    for i in range(0, sizes[0], 2):
        for j in range(0, sizes[1], 2):
            for k in range(0, sizes[2], 2):
                members = []
                for a, b, c in RELATIVE:
                    x = (i + a + offsets[0]) % sizes[0]
                    y = (j + b + offsets[1]) % sizes[1]
                    z = (k + c + offsets[2]) % sizes[2]
                    members.append((x * sizes[1] + y) * sizes[2] + z)
                groups.append(members)
    return groups


def swap(chunks, side):
    sizes = [lax.axis_size(axis) for axis in AXES]
    return lax.all_to_all(chunks, AXES, 0, 0, axis_index_groups=bricks(sizes, OFFSETS[side]))


def shared(r, side):
    return [v for v, e in enumerate(RELATIVE) if all(e[d] == side for d in range(3) if RELATIVE[r][d])]


def near(r, side):
    return [v for v, e in enumerate(RELATIVE) if any(e[d] == side for d in range(3) if RELATIVE[r][d])]


def runs(corners):
    out = []
    for k, v in enumerate(corners):
        if out and out[-1][1] + out[-1][2] == NP * v:
            out[-1][2] += NP
        else:
            out.append([NP * k, NP * v, NP])
    return out


def face_nodes(r, side):
    x, y, z = RELATIVE[r]
    f = PDEG * side
    out = np.full(64, -1, np.int32)

    def row(a, b, c):
        return (a * SIDE + b) * ROW + c

    free = [d for d in range(3) if not RELATIVE[r][d]]
    if len(free) == 2:
        for i in range(SIDE):
            for j in range(SIDE):
                at = [f, f, f]
                at[free[0]], at[free[1]] = i, j
                out[8 * i + j] = row(*at)
    elif len(free) == 1:
        for i in range(SIDE):
            at = [f, f, f]
            at[free[0]] = i
            out[i] = row(*at)
    else:
        out[0] = row(f, f, f)
    return out


@functools.cache
def lane_tables(side):
    low = np.full((8, 128), -1, np.int32)
    high = np.full((8, 128), -1, np.int32)
    for r in range(1, 8):
        low[r, :64] = face_nodes(r, side)
        high[r, 64:] = face_nodes(r, side)
    return low, high


@functools.cache
def corner_table(side):
    table = np.full((CP + 7 * CHUNK, 8), -1, np.int32)

    def fill(first, lattice):
        for s, bits in enumerate(RELATIVE):
            corner = [2 * side - u if bit else u for u, bit in zip(lattice, bits)]
            if all(c in (0, 1) for c in corner):
                v = 4 * corner[0] + 2 * corner[1] + corner[2]
                table[first : first + NP, s] = NP * v + np.arange(NP)

    for v, e in enumerate(RELATIVE):
        fill(NP * v, e)
    for r in range(1, 8):
        for k, v in enumerate(near(r, side)):
            lattice = [2 * side - e if bit else e for e, bit in zip(RELATIVE[v], RELATIVE[r])]
            fill(CP + (r - 1) * CHUNK + NP * k, lattice)
    return table


def node_masks(side):
    masks = np.ones((8, NODES), np.float32)
    for r in range(1, 8):
        nodes = face_nodes(r, side)
        masks[r, nodes[nodes >= 0]] = 0.0
    return masks


def add_faces(ref, part, r, side, face=FACE, edge=EDGE, last=LAST):
    f = PDEG * side
    if r == 4:
        rows = pl.ds(f * SIDE * ROW, SIDE * ROW)
        ref[rows, :] = ref[rows, :] + part(face, SIDE * ROW)
    elif r == 2:
        for a in range(SIDE):
            rows = pl.ds((a * SIDE + f) * ROW, ROW)
            ref[rows, :] = ref[rows, :] + part(face + ROW * a, ROW)
    elif r == 1:
        rows = pl.ds(f, SIDE * SIDE, ROW)
        ref[rows, :] = ref[rows, :] + part(face, SIDE * SIDE)
    elif r == 6:
        rows = pl.ds((f * SIDE + f) * ROW, ROW)
        ref[rows, :] = ref[rows, :] + part(edge, ROW)
    elif r == 5:
        rows = pl.ds(f * SIDE * ROW + f, SIDE, ROW)
        ref[rows, :] = ref[rows, :] + part(edge, SIDE)
    elif r == 3:
        rows = pl.ds(f * ROW + f, SIDE, SIDE * ROW)
        ref[rows, :] = ref[rows, :] + part(edge, SIDE)
    else:
        rows = pl.ds((f * SIDE + f) * ROW + f, 1)
        ref[rows, :] = ref[rows, :] + part(last, 1)


def put_faces(ref, put, r, side, face=FACE, edge=EDGE, last=LAST):
    f = PDEG * side
    if r == 4:
        put(face, SIDE * ROW, ref[pl.ds(f * SIDE * ROW, SIDE * ROW), :])
    elif r == 2:
        for a in range(SIDE):
            put(face + ROW * a, ROW, ref[pl.ds((a * SIDE + f) * ROW, ROW), :])
    elif r == 1:
        put(face, SIDE * SIDE, ref[pl.ds(f, SIDE * SIDE, ROW), :])
    elif r == 6:
        put(edge, ROW, ref[pl.ds((f * SIDE + f) * ROW, ROW), :])
    elif r == 5:
        put(edge, SIDE, ref[pl.ds(f * SIDE * ROW + f, SIDE, ROW), :])
    elif r == 3:
        put(edge, SIDE, ref[pl.ds(f * ROW + f, SIDE, SIDE * ROW), :])
    else:
        put(last, 1, ref[pl.ds((f * SIDE + f) * ROW + f, 1), :])


def loader(ref, slot):
    return lambda first, rows: ref[slot, pl.ds(first, rows), :]


def storer(ref, slot):
    def put(first, rows, value):
        ref[slot, pl.ds(first, rows), :] = value

    return put


def dot(a, b):
    if INTERPRET:
        a, b = a.astype(jnp.float32), b.astype(jnp.float32)
    return jnp.dot(a, b, preferred_element_type=jnp.float32)


def open_kernel(me_ref, beta_ref, y_ref, xl_ref, xh_ref, yl_ref, yh_ref, p_ref, sx_ref, sy_ref):
    me = me_ref[0]
    p_ref[...] = dot(beta_ref[...], y_ref[...])
    row = lax.broadcasted_iota(jnp.int32, (NODES, 128), 0)
    zeros = jnp.zeros((FACE, W), jnp.float32)
    sx_ref[me] = jnp.zeros((2 * FACE, W), jnp.float32)
    sy_ref[7 - me] = zeros
    for r in range(1, 8):
        slot = me ^ r
        for first, at, rows in runs(shared(r, 1)):
            sx_ref[slot, pl.ds(first, rows), :] = p_ref[pl.ds(at, rows), :]
        used = NP * len(shared(r, 1))
        if used < FACE:
            sx_ref[slot, pl.ds(used, FACE - used), :] = jnp.zeros((FACE - used, W), jnp.float32)
        for low_ref, high_ref, out_ref, to, first in (
            (xl_ref, xh_ref, sx_ref, slot, FACE),
            (yl_ref, yh_ref, sy_ref, (7 - me) ^ r, 0),
        ):
            low = (row == low_ref[pl.ds(r, 1), :]).astype(jnp.float32).astype(jnp.bfloat16)
            high = (row == high_ref[pl.ds(r, 1), :]).astype(jnp.float32).astype(jnp.bfloat16)
            packed = dot(beta_ref[pl.ds(0, FACE), :], low) + dot(beta_ref[pl.ds(FACE, FACE), :], high)
            out_ref[to, pl.ds(first, FACE), :] = packed


def assemble_kernel(first, flip, me_ref, in_ref, beta_ref, low_ref, high_ref, table_ref, mask_ref, own_ref, far_ref, acc_ref):
    me = me_ref[0] ^ flip
    lane = lax.broadcasted_iota(jnp.int32, (128, NODES), 1)
    pick = lax.broadcasted_iota(jnp.int32, (CP + 7 * CHUNK, CP), 1)

    def chosen(s):
        return (pick == table_ref[:, pl.ds(s, 1)]).astype(jnp.float32).astype(jnp.bfloat16)

    acc_ref[...] = dot(chosen(0), beta_ref[...])
    for s in range(1, 8):
        packed = in_ref[me ^ s, pl.ds(first, FACE), :].astype(jnp.bfloat16)
        low = (lane == low_ref[:, pl.ds(s, 1)]).astype(jnp.float32).astype(jnp.bfloat16)
        high = (lane == high_ref[:, pl.ds(s, 1)]).astype(jnp.float32).astype(jnp.bfloat16)
        spread = jnp.concatenate([dot(packed, low), dot(packed, high)], axis=0).astype(jnp.bfloat16)
        acc_ref[...] = acc_ref[...] + dot(chosen(s), spread)
    own_ref[...] = acc_ref[pl.ds(0, CP), :].astype(jnp.bfloat16)
    for r in range(1, 8):
        block = acc_ref[pl.ds(CP + (r - 1) * CHUNK, CHUNK), :] * mask_ref[pl.ds(r, 1), :]
        far_ref[pl.ds((r - 1) * CHUNK, CHUNK), :] = block.astype(jnp.bfloat16)


def send_terms(me, corr_ref, coupling_ref, ham_ref, y, own_ref, c_ref, f_ref, send_ref):
    c_ref[...] = jnp.dot(
        coupling_ref[...], corr_ref[...], precision=lax.Precision.HIGHEST, preferred_element_type=jnp.float32
    )
    f_ref[...] = dot(ham_ref[...], y) + dot(own_ref[...], c_ref[...].astype(jnp.bfloat16))
    send_ref[me] = jnp.zeros((CHUNK, W), jnp.float32)
    for r in range(1, 8):
        slot = me ^ r
        corners = near(r, 0)
        used = NP * len(corners)
        if used != FACE:
            send_ref[slot, pl.ds(used // 8 * 8, CHUNK - used // 8 * 8), :] = jnp.zeros(
                (CHUNK - used // 8 * 8, W), jnp.float32
            )
        for first, at, rows in runs(corners):
            send_ref[slot, pl.ds(first, rows), :] = c_ref[pl.ds(at, rows), :]
        if r == 1:
            send_ref[slot, pl.ds(FACE + 48, 8), :] = jnp.zeros((8, W), jnp.float32)
        put_faces(f_ref, storer(send_ref, slot), r, 0)


def first_kernel(me_ref, in_ref, p_ref, y_ref, coupling_ref, ham_ref, own_ref, f_ref, send_ref, corr_ref, c_ref):
    me = me_ref[0]
    corr_ref[...] = p_ref[...]
    for r in range(1, 8):
        for first, at, rows in runs(shared(r, 1)):
            corr_ref[pl.ds(at, rows), :] = corr_ref[pl.ds(at, rows), :] + in_ref[me ^ r, pl.ds(first, rows), :]
    send_terms(7 - me, corr_ref, coupling_ref, ham_ref, y_ref[...], own_ref, c_ref, f_ref, send_ref)


def vertex_kernel(
    me_ref, in_ref, z_ref, ownx_ref, coupling_ref, ham_ref, owny_ref, y_ref, f_ref, send_ref, t_ref, corr_ref, c_ref
):
    me = me_ref[0]
    t_ref[...] = z_ref[...]
    for r in range(1, 8):
        add_faces(t_ref, loader(in_ref, me ^ r), r, 1)
    y = t_ref[...].astype(jnp.bfloat16)
    y_ref[...] = y
    corr_ref[...] = dot(ownx_ref[...], y)
    for r in range(1, 8):
        for first, at, rows in runs(near(r, 1)):
            corr_ref[pl.ds(at, rows), :] = corr_ref[pl.ds(at, rows), :] + in_ref[me ^ r, pl.ds(first, rows), :]
    send_terms(7 - me, corr_ref, coupling_ref, ham_ref, y, owny_ref, c_ref, f_ref, send_ref)


def node_kernel(scales, final, me_ref, in_ref, f_ref, fary_ref, y_ref, before_ref, share_ref, farx_ref, z_ref, send_ref, a_ref, t_ref):
    me = me_ref[0]
    for r in range(1, 8):
        a_ref[pl.ds((r - 1) * CHUNK, CHUNK), :] = in_ref[(7 - me) ^ r].astype(jnp.bfloat16)
    t_ref[...] = f_ref[...] + dot(fary_ref[...], a_ref[...])
    for r in range(1, 8):
        add_faces(t_ref, loader(in_ref, (7 - me) ^ r), r, 0)
    applied, now, before = scales
    kept = now * y_ref[...].astype(jnp.float32)
    if before:
        kept = kept + before * before_ref[...].astype(jnp.float32)
    z_ref[...] = applied * t_ref[...] + share_ref[...] * kept
    if final:
        send_ref[...] = jnp.zeros_like(send_ref)
        for r in range(1, 8):
            put_faces(z_ref, storer(send_ref, me ^ r), r, 1, 0, 0, 0)
        return
    z = z_ref[...].astype(jnp.bfloat16)
    send_ref[me] = jnp.zeros((CHUNK, W), jnp.float32)
    for r in range(1, 8):
        send_ref[me ^ r] = dot(farx_ref[pl.ds((r - 1) * CHUNK, CHUNK), :], z)
        put_faces(z_ref, storer(send_ref, me ^ r), r, 1)


def close_kernel(me_ref, in_ref, z_ref, mirror_ref, out_ref, t_ref):
    me = me_ref[0]
    t_ref[...] = z_ref[...]
    for r in range(1, 8):
        add_faces(t_ref, loader(in_ref, me ^ r), r, 1, 0, 0, 0)
    out_ref[...] = dot(mirror_ref[...], t_ref[...].astype(jnp.bfloat16)).astype(jnp.bfloat16)


def call(kernel, me, inputs, outs, scratch=()):
    smem = pl.BlockSpec(memory_space=pltpu.SMEM)
    vmem = pl.BlockSpec(memory_space=pltpu.VMEM)
    return pl.pallas_call(
        kernel,
        out_shape=[jax.ShapeDtypeStruct(shape, dtype) for shape, dtype in outs],
        in_specs=[smem] + [vmem] * len(inputs),
        out_specs=[vmem] * len(outs),
        scratch_shapes=[pltpu.VMEM(shape, dtype) for shape, dtype in scratch],
        interpret=INTERPRET,
    )(me, *inputs)


def mirrored(values, flips):
    for d in range(3):
        values = jnp.where(flips[d], jnp.flip(values, d), values)
    return values


def exact_dot(a, b, dims):
    return lax.dot_general(a, b, (dims, ((), ())), preferred_element_type=jnp.float32).astype(a.dtype)


def local(wavefunctions, cell_hamiltonian, projectors, atom_species, coupling):
    node_count = cell_hamiltonian.shape[3]
    sizes = [lax.axis_size(axis) for axis in AXES]
    bits = [(lax.axis_index(axis) + sizes[d] - OFFSETS[1][d]) % 2 for d, axis in enumerate(AXES)]
    flips = [bit == 1 for bit in bits]
    me = (4 * bits[0] + 2 * bits[1] + bits[2]).astype(jnp.int32).reshape(1)

    def mirror_of(shape, padded_dim):
        padded = lax.broadcasted_iota(jnp.int32, shape, padded_dim)
        plain = lax.broadcasted_iota(jnp.int32, shape, 1 - padded_dim)
        place = [padded // (SIDE * ROW), (padded // ROW) % SIDE, padded % ROW]
        inside = place[2] < SIDE
        place = [jnp.where(f, PDEG - p, p) for f, p in zip(flips, place)]
        same = plain == (place[0] * SIDE + place[1]) * SIDE + place[2]
        return jnp.logical_and(same, inside).astype(jnp.bfloat16)

    into = mirror_of((NODES, node_count), 0)
    back = mirror_of((node_count, NODES), 1)
    ham = exact_dot(into, cell_hamiltonian.reshape(node_count, node_count), ((1,), (0,)))
    ham = exact_dot(ham, back, ((1,), (0,)))
    betas = mirrored(projectors.reshape(2, 2, 2, NP, node_count), flips).reshape(CP, node_count)
    betas = exact_dot(betas, back, ((1,), (0,)))
    current = exact_dot(into, wavefunctions.reshape(node_count, W), ((1,), (0,)))

    species = mirrored(atom_species, flips).reshape(8)
    kinds = jnp.arange(1, coupling.shape[0] + 1, dtype=jnp.int32)
    mask = (species[:, None] == kinds).astype(jnp.float32)
    per_corner = jnp.einsum("vs,spq->vpq", mask, coupling, precision=lax.Precision.HIGHEST)
    blocks = jnp.tile(per_corner.reshape(CP, NP), (1, 8))
    corner_of = jnp.arange(CP) // NP
    blocks = jnp.where(corner_of[:, None] == corner_of[None, :], blocks, 0.0)

    f32, bf16 = jnp.float32, jnp.bfloat16
    (xl, xh), (yl, yh) = lane_tables(1), lane_tables(0)
    p, sx, sy = call(
        open_kernel,
        me,
        (betas, current, xl, xh, yl, yh),
        [((CP, W), f32), ((8, 2 * FACE, W), f32), ((8, FACE, W), f32)],
    )
    ax = swap(sx, 1)
    ay = swap(sy, 0)

    def assemble(side, arrived, first):
        low, high = lane_tables(side)
        return call(
            functools.partial(assemble_kernel, first, 0 if side else 7),
            me,
            (arrived, betas, low.T.copy(), high.T.copy(), corner_table(side), node_masks(side)),
            [((CP, NODES), bf16), ((7 * CHUNK, NODES), bf16)],
            [((CP + 7 * CHUNK, NODES), f32)],
        )

    ownx, farx = assemble(1, ax, FACE)
    owny, fary = assemble(0, ay, 0)
    owny, fary = owny.T, fary.T

    node = np.arange(NODES)
    place = [node // (SIDE * ROW), (node // ROW) % SIDE, node % ROW]
    share = np.prod([np.where(q == PDEG, 0.5, 1.0) for q in place], axis=0).astype(np.float32).reshape(NODES, 1)

    packet = ((8, CHUNK, W), f32)
    plane = (NODES, W)
    f, send = call(
        first_kernel, me, (ax, p, current, blocks, ham, owny), [(plane, f32), packet], [((CP, W), f32)] * 2
    )
    previous = current
    for step in range(ORDER):
        final = step == ORDER - 1
        arrived = swap(send, 0)
        scales = (1.0 / HALF, -CENTER / HALF, 0.0) if step == 0 else (2.0 / HALF, -2.0 * CENTER / HALF, -1.0)
        z, send = call(
            functools.partial(node_kernel, scales, final),
            me,
            (arrived, f, fary, current, previous, share, farx),
            [(plane, f32), ((8, 56, W), f32) if final else packet],
            [((7 * CHUNK, W), bf16), (plane, f32)],
        )
        arrived = swap(send, 1)
        if final:
            (out,) = call(close_kernel, me, (arrived, z, back), [((node_count, W), bf16)], [(plane, f32)])
            return out.reshape(wavefunctions.shape)
        previous = current
        current, f, send = call(
            vertex_kernel,
            me,
            (arrived, z, ownx, blocks, ham, owny),
            [(plane, bf16), (plane, f32), packet],
            [(plane, f32), ((CP, W), f32), ((CP, W), f32)],
        )


def solution(mesh):
    placed = (
        P("gx", "gy", "gz", None),
        P("gx", "gy", "gz", None, None),
        P("gx", "gy", "gz", None, None, None),
        P("gx", "gy", "gz"),
        P(),
    )
    return jax.shard_map(
        local, mesh=mesh, in_specs=placed, out_specs=P("gx", "gy", "gz", None), check_vma=False
    )
```

time: 328 us -> 239 us (0.73)
  local copies, waits for them, and re-layouts: 78.1 us -> 9.74 us
  Pallas kernels: 0 us -> 43.7 us
  starting transfers between devices: 54.3 us -> 23.3 us
  blocking collectives: 159 us -> 137 us
  waiting for transfers between devices: 19.8 us -> 14.2 us
  between operations: 4.49 us -> 0.18 us
  matrix products: 7.87 us -> 4.37 us
    unnamed x343 -> x17, local copies, waits for them, and re-layouts: 50.4 us -> 3.72 us
    pallas_call x0 -> x12, Pallas kernels: none -> 43.7 us  [call(): pl.pallas_call(kernel, out_shape=[jax.ShapeDtypeStruct(shape, dtype) for...]
    all_to_all x5 -> x3, starting transfers between devices: 54.3 us -> 23.3 us  [swap(): lax.all_to_all(chunks, AXES, 0, 0, axis_index_groups=bricks(sizes, OFFSET...]
    all_to_all x11 -> x7, blocking collectives: 159 us -> 137 us  [swap(): lax.all_to_all(chunks, AXES, 0, 0, axis_index_groups=bricks(sizes, OFFSET...]
    slice x140 -> x0, local copies, waits for them, and re-layouts: 17.4 us -> none  [the longest x120 16.6 us: side_slice(): values = lax.slice_in_dim(values, index, index + 1, axis=d)]
    all_to_all x5 -> x3, waiting for transfers between devices: 19.8 us -> 14.2 us  [swap(): lax.all_to_all(chunks, AXES, 0, 0, axis_index_groups=bricks(sizes, OFFSET...]
    dot_general x17 -> x1, matrix products: 4.84 us -> 0.29 us  [local(): jnp.einsum('vs,spq->vpq', mask, coupling, precision=lax.Precision.HIGHEST)]
    another operation x53 -> x4, local copies, waits for them, and re-layouts: 3.95 us -> 0.22 us  [local(): blocks = jnp.tile(per_corner.reshape(CP, NP), (1, 8))]
  transfers between devices with their start and end apart: 5 -> 3, of which waited for: 5 -> 2; matrix products, arithmetic and copies ran while one was open for 2% -> 3% of each run, Pallas kernels for 0% -> 5%
where the time goes in v2:
time: 239 us; the launch traced here: 234 us
  blocking collectives  137 us (57%)
  Pallas kernels  43.7 us (18%)
  starting transfers between devices  23.3 us (10%)
  waiting for transfers between devices  14.2 us (6%)
  local copies, waits for them, and re-layouts  9.74 us (4%)
  matrix products  4.37 us (2%)
    all_to_all x7, blocking collectives, swap(): lax.all_to_all(chunks, AXES, 0, 0, axis_index_groups=bricks(sizes, OFFSET...  137 us
    pallas_call x12, Pallas kernels, call(): pl.pallas_call(kernel, out_shape=[jax.ShapeDtypeStruct(shape, dtype) for...  43.7 us
    all_to_all x3, starting transfers between devices, swap(): lax.all_to_all(chunks, AXES, 0, 0, axis_index_groups=bricks(sizes, OFFSET...  23.3 us
    all_to_all x3, waiting for transfers between devices, swap(): lax.all_to_all(chunks, AXES, 0, 0, axis_index_groups=bricks(sizes, OFFSET...  14.2 us
  transfers between devices with their start and end apart: 3, of which 2 were waited for; matrix products, arithmetic and copies ran while one was open for 3% of the time, Pallas kernels for 5%

profile of v2, /device:TPU:1, one launch (start us, length us, event | category | flops | bytes accessed | tf_op | source)
XLA Modules:
  0.0 234.5 jit_solution(1569764121853967224)
XLA Ops:
  4.4 2.7 %shard_map.172 = (f32[144,128]{1,0:T(8,128)}, f32[8,144,128]{2,1,0:T(8,128)}, f32[8,72,128]{2,1,0:T(8,128)}) custom-call(s32[1]{0:T(128)} %bitcast.me_ref, bf16[144,392]{1,0:T(8,128)(2,1)} %convolution_convert_fusion.2.beta_ref, bf16[392,128]{1,0:T(8,128)(2,1)} %convolution_convert_fusion.3.y_ref.before_ref, s32[8,128]{1,0:T(8,128)} %constant.150.clone.xl_ref, ...), custom_call_target="tpu_custom_call" | custom-call | tf_op jit(solution)/shard_map/pallas_call | solution.py:324
  7.0 24.2 %all_to_all.50.in_ref = f32[8,72,128]{2,1,0:T(8,128)} all-to-all(f32[8,72,128]{2,1,0:T(8,128)} %get-tuple-element.33), channel_id=1, replica_groups={{17,18,33,34,145,146,161,162},{19,20,35,36,147,148,163,164},{21,22,37,3..., dimensions={0} | all-to-all | bytes 589824 | tf_op jit(solution)/shard_map/all_to_all | solution.py:52
  31.2 7.1 %all-to-all-start = ((f32[8,144,128]{2,1,0:T(8,128)}), f32[8,144,128]{2,1,0:T(8,128)S(1)}, u32[]{:S(2)}, u32[]{:S(2)}) async-start(f32[8,144,128]{2,1,0:T(8,128)} %get-tuple-element.31), calls=%async_computation | async-start | bytes 1179648 | tf_op jit(solution)/shard_map/all_to_all | solution.py:52
  42.3 6.1 %shard_map.173 = (bf16[144,392]{1,0:T(8,128)(2,1)}, bf16[896,392]{1,0:T(8,128)(2,1)}) custom-call(s32[1]{0:T(128)} %bitcast.me_ref, f32[8,72,128]{2,1,0:T(8,128)} %all_to_all.50.in_ref, bf16[144,392]{1,0:T(8,128)(2,1)} %convolution_convert_fusion.2.beta_ref, s32[128,8]{1,0:T(8,128)} %constant.158.clone.low_ref, s32[128,8]{1,0:T(8,128)} %constant.159.clone.high_ref, ...), custom_call_target="tpu_custom_call" | custom-call | tf_op jit(solution)/shard_map/pallas_call | solution.py:324
  50.1 4.8 %all-to-all-done.in_ref = f32[8,144,128]{2,1,0:T(8,128)S(1)} async-done(((f32[8,144,128]{2,1,0:T(8,128)}), f32[8,144,128]{2,1,0:T(8,128)S(1)}, u32[]{:S(2)}, u32[]{:S(2)}) %all-to-all-start) | async-done | bytes 589856 | tf_op jit(solution)/shard_map/all_to_all | solution.py:52
  55.7 3.1 %shard_map.174 = (f32[392,128]{1,0:T(8,128)}, f32[8,128,128]{2,1,0:T(8,128)}) custom-call(s32[1]{0:T(128)} %bitcast.me_ref, f32[8,144,128]{2,1,0:T(8,128)} %copy-done.1, f32[144,128]{1,0:T(8,128)} %get-tuple-element.32.p_ref, bf16[392,128]{1,0:T(8,128)(2,1)} %convolution_convert_fusion.3.y_ref.before_ref, f32[144,144]{1,0:T(8,128)} %compare_select_fusion.coupling_ref, ...), custom_call_target="tpu_custom_call" | custom-call | tf_op jit(solution)/shard_map/pallas_call | solution.py:324
  58.8 12.0 %all-to-all-start.2 = ((f32[8,128,128]{2,1,0:T(8,128)}), f32[8,128,128]{2,1,0:T(8,128)S(1)}, u32[]{:S(2)}, u32[]{:S(2)}) async-start(f32[8,128,128]{2,1,0:T(8,128)} %get-tuple-element.35), calls=%async_computation.2 | async-start | bytes 1048576 | tf_op jit(solution)/shard_map/all_to_all | solution.py:52
  72.1 6.2 %shard_map.175 = (bf16[144,392]{1,0:T(8,128)(2,1)}, bf16[896,392]{1,0:T(8,128)(2,1)}) custom-call(s32[1]{0:T(128)} %bitcast.me_ref, f32[8,144,128]{2,1,0:T(8,128)} %copy-done.1, bf16[144,392]{1,0:T(8,128)(2,1)} %convolution_convert_fusion.2.beta_ref, s32[128,8]{1,0:T(8,128)} %constant.154.clone.low_ref, s32[128,8]{1,0:T(8,128)} %constant.155.clone.high_ref, ...), custom_call_target="tpu_custom_call" | custom-call | tf_op jit(solution)/shard_map/pallas_call | solution.py:324
  79.1 3.5 %shard_map.176 = (f32[392,128]{1,0:T(8,128)}, f32[8,128,128]{2,1,0:T(8,128)}) custom-call(s32[1]{0:T(128)} %bitcast.me_ref, f32[8,128,128]{2,1,0:T(8,128)} %copy-done.2, f32[392,128]{1,0:T(8,128)} %get-tuple-element.36.f_ref, bf16[392,896]{1,0:T(8,128)(2,1)} %bitcast.18, bf16[392,128]{1,0:T(8,128)(2,1)} %convolution_convert_fusion.3.y_ref.before_ref, ...), custom_call_target="tpu_custom_call" | custom-call | tf_op jit(solution)/shard_map/pallas_call | solution.py:324
  82.6 21.7 %all_to_all.51.in_ref = f32[8,128,128]{2,1,0:T(8,128)} all-to-all(f32[8,128,128]{2,1,0:T(8,128)} %get-tuple-element.39), channel_id=1, replica_groups={{128,129,144,145,256,257,272,273},{130,131,146,147,258,259,274,275},{13..., dimensions={0} | all-to-all | bytes 1048576 | tf_op jit(solution)/shard_map/all_to_all | solution.py:52
  104.3 3.3 %shard_map.177 = (bf16[392,128]{1,0:T(8,128)(2,1)}, f32[392,128]{1,0:T(8,128)}, f32[8,128,128]{2,1,0:T(8,128)}) custom-call(s32[1]{0:T(128)} %bitcast.me_ref, f32[8,128,128]{2,1,0:T(8,128)} %all_to_all.51.in_ref, f32[392,128]{1,0:T(8,128)} %get-tuple-element.40.z_ref, bf16[144,392]{1,0:T(8,128)(2,1)} %get-tuple-element.41.ownx_ref, ...), custom_call_target="tpu_custom_call" | custom-call | tf_op jit(solution)/shard_map/pallas_call | solution.py:324
  107.6 16.5 %all_to_all.52.in_ref = f32[8,128,128]{2,1,0:T(8,128)} all-to-all(f32[8,128,128]{2,1,0:T(8,128)} %get-tuple-element.42), channel_id=1, replica_groups={{17,18,33,34,145,146,161,162},{19,20,35,36,147,148,163,164},{21,22,37,3..., dimensions={0} | all-to-all | bytes 1048576 | tf_op jit(solution)/shard_map/all_to_all | solution.py:52
  124.1 3.5 %shard_map.178 = (f32[392,128]{1,0:T(8,128)}, f32[8,128,128]{2,1,0:T(8,128)}) custom-call(s32[1]{0:T(128)} %bitcast.me_ref, f32[8,128,128]{2,1,0:T(8,128)} %all_to_all.52.in_ref, f32[392,128]{1,0:T(8,128)} %get-tuple-element.43.f_ref, bf16[392,896]{1,0:T(8,128)(2,1)} %bitcast.19, bf16[392,128]{1,0:T(8,128)(2,1)} %get-tuple-element.44.y_ref.before_ref, ...), custom_call_target="tpu_custom_call" | custom-call | tf_op jit(solution)/shard_map/pallas_call | solution.py:324
  127.6 20.2 %all_to_all.53.in_ref = f32[8,128,128]{2,1,0:T(8,128)} all-to-all(f32[8,128,128]{2,1,0:T(8,128)} %get-tuple-element.45), channel_id=1, replica_groups={{128,129,144,145,256,257,272,273},{130,131,146,147,258,259,274,275},{13..., dimensions={0} | all-to-all | bytes 1048576 | tf_op jit(solution)/shard_map/all_to_all | solution.py:52
  147.8 3.3 %shard_map.179 = (bf16[392,128]{1,0:T(8,128)(2,1)}, f32[392,128]{1,0:T(8,128)}, f32[8,128,128]{2,1,0:T(8,128)}) custom-call(s32[1]{0:T(128)} %bitcast.me_ref, f32[8,128,128]{2,1,0:T(8,128)} %all_to_all.53.in_ref, f32[392,128]{1,0:T(8,128)} %get-tuple-element.46.z_ref, bf16[144,392]{1,0:T(8,128)(2,1)} %get-tuple-element.41.ownx_ref, ...), custom_call_target="tpu_custom_call" | custom-call | tf_op jit(solution)/shard_map/pallas_call | solution.py:324
  151.1 17.0 %all_to_all.54.in_ref = f32[8,128,128]{2,1,0:T(8,128)} all-to-all(f32[8,128,128]{2,1,0:T(8,128)} %get-tuple-element.47), channel_id=1, replica_groups={{17,18,33,34,145,146,161,162},{19,20,35,36,147,148,163,164},{21,22,37,3..., dimensions={0} | all-to-all | bytes 1048576 | tf_op jit(solution)/shard_map/all_to_all | solution.py:52
  168.1 3.5 %shard_map.180 = (f32[392,128]{1,0:T(8,128)}, f32[8,128,128]{2,1,0:T(8,128)}) custom-call(s32[1]{0:T(128)} %bitcast.me_ref, f32[8,128,128]{2,1,0:T(8,128)} %all_to_all.54.in_ref, f32[392,128]{1,0:T(8,128)} %get-tuple-element.48.f_ref, bf16[392,896]{1,0:T(8,128)(2,1)} %bitcast.20, bf16[392,128]{1,0:T(8,128)(2,1)} %get-tuple-element.49.y_ref.before_ref, ...), custom_call_target="tpu_custom_call" | custom-call | tf_op jit(solution)/shard_map/pallas_call | solution.py:324
  171.6 20.1 %all_to_all.55.in_ref = f32[8,128,128]{2,1,0:T(8,128)} all-to-all(f32[8,128,128]{2,1,0:T(8,128)} %get-tuple-element.50), channel_id=1, replica_groups={{128,129,144,145,256,257,272,273},{130,131,146,147,258,259,274,275},{13..., dimensions={0} | all-to-all | bytes 1048576 | tf_op jit(solution)/shard_map/all_to_all | solution.py:52
  191.7 3.3 %shard_map.181 = (bf16[392,128]{1,0:T(8,128)(2,1)}, f32[392,128]{1,0:T(8,128)}, f32[8,128,128]{2,1,0:T(8,128)}) custom-call(s32[1]{0:T(128)} %bitcast.me_ref, f32[8,128,128]{2,1,0:T(8,128)} %all_to_all.55.in_ref, f32[392,128]{1,0:T(8,128)} %get-tuple-element.51.z_ref, bf16[144,392]{1,0:T(8,128)(2,1)} %get-tuple-element.41.ownx_ref, ...), custom_call_target="tpu_custom_call" | custom-call | tf_op jit(solution)/shard_map/pallas_call | solution.py:324
  195.0 17.5 %all_to_all.56.in_ref = f32[8,128,128]{2,1,0:T(8,128)} all-to-all(f32[8,128,128]{2,1,0:T(8,128)} %get-tuple-element.52), channel_id=1, replica_groups={{17,18,33,34,145,146,161,162},{19,20,35,36,147,148,163,164},{21,22,37,3..., dimensions={0} | all-to-all | bytes 1048576 | tf_op jit(solution)/shard_map/all_to_all | solution.py:52
  212.5 3.1 %shard_map.182 = (f32[392,128]{1,0:T(8,128)}, f32[8,56,128]{2,1,0:T(8,128)}) custom-call(s32[1]{0:T(128)} %bitcast.me_ref, f32[8,128,128]{2,1,0:T(8,128)} %all_to_all.56.in_ref, f32[392,128]{1,0:T(8,128)} %get-tuple-element.53.f_ref, bf16[392,896]{1,0:T(8,128)(2,1)} %bitcast.21, bf16[392,128]{1,0:T(8,128)(2,1)} %get-tuple-element.54.y_ref, ...), custom_call_target="tpu_custom_call" | custom-call | tf_op jit(solution)/shard_map/pallas_call | solution.py:324
  215.6 4.2 %all-to-all-start.9 = ((f32[8,56,128]{2,1,0:T(8,128)}), f32[8,56,128]{2,1,0:T(8,128)S(1)}, u32[]{:S(2)}, u32[]{:S(2)}) async-start(f32[8,56,128]{2,1,0:T(8,128)} %get-tuple-element.55), calls=%async_computation.9 | async-start | bytes 458752 | tf_op jit(solution)/shard_map/all_to_all | solution.py:52
  220.7 9.4 %all-to-all-done.9.in_ref = f32[8,56,128]{2,1,0:T(8,128)S(1)} async-done(((f32[8,56,128]{2,1,0:T(8,128)}), f32[8,56,128]{2,1,0:T(8,128)S(1)}, u32[]{:S(2)}, u32[]{:S(2)}) %all-to-all-start.9) | async-done | bytes 229408 | tf_op jit(solution)/shard_map/all_to_all | solution.py:52
  230.8 2.1 shard_map.183
  (50 shorter events, 15.9 us)
Async XLA Ops:
  0.0 40.5 %copy-start = (bf16[1,1,1,343,343]{4,3,2,1,0:T(8,128)(2,1)S(1)}, bf16[1,1,1,343,343]{4,3,2,1,0:T(8,128)(2,1)}, u32[]{:S(2)}) copy-start(bf16[1,1,1,343,343]{4,3,2,1,0:T(8,128)(2,1)} %param.19) | copy-start | bytes 705898
  1.1 0.9 copy-start.5
  31.2 7.1 %copy-start.7 = (s32[2,2,2]{2,1,0:T(2,128)S(1)}, s32[2,2,2]{2,1,0:T(2,128)}, u32[]{:S(2)}) copy-start(s32[2,2,2]{2,1,0:T(2,128)} %param.21) | copy-start | bytes 100
  31.2 23.6 %all-to-all-start = ((f32[8,144,128]{2,1,0:T(8,128)}), f32[8,144,128]{2,1,0:T(8,128)S(1)}, u32[]{:S(2)}, u32[]{:S(2)}) async-start(f32[8,144,128]{2,1,0:T(8,128)} %get-tuple-element.31), calls=%async_computation | async-start | bytes 1179648 | tf_op jit(solution)/shard_map/all_to_all | solution.py:52
  38.4 0.7 copy-start.6
  54.9 0.8 copy-start.1
  55.7 15.2 %copy-start.3 = (bf16[896,392]{1,0:T(8,128)(2,1)S(1)}, bf16[896,392]{1,0:T(8,128)(2,1)}, u32[]{:S(2)}) copy-start(bf16[896,392]{1,0:T(8,128)(2,1)} %get-tuple-element.37) | copy-start | bytes 2107396
  58.8 19.5 %all-to-all-start.2 = ((f32[8,128,128]{2,1,0:T(8,128)}), f32[8,128,128]{2,1,0:T(8,128)S(1)}, u32[]{:S(2)}, u32[]{:S(2)}) async-start(f32[8,128,128]{2,1,0:T(8,128)} %get-tuple-element.35), calls=%async_computation.2 | async-start | bytes 1048576 | tf_op jit(solution)/shard_map/all_to_all | solution.py:52
  78.3 0.8 copy-start.2
  215.6 14.5 %all-to-all-start.9 = ((f32[8,56,128]{2,1,0:T(8,128)}), f32[8,56,128]{2,1,0:T(8,128)S(1)}, u32[]{:S(2)}, u32[]{:S(2)}) async-start(f32[8,56,128]{2,1,0:T(8,128)} %get-tuple-element.55), calls=%async_computation.9 | async-start | bytes 458752 | tf_op jit(solution)/shard_map/all_to_all | solution.py:52
  230.1 0.7 copy-start.4

commit v3 on v2

--- a/solution.py
+++ b/solution.py
@@ -26,6 +26,7 @@
 FACE = 72
 EDGE = 112
 LAST = 127
+LIMIT = 12 << 20
 
 AXES = ("gx", "gy", "gz")
 OFFSETS = {1: (1, 0, 0), 0: (0, 1, 1)}
@@ -103,6 +104,23 @@
         low[r, :64] = face_nodes(r, side)
         high[r, 64:] = face_nodes(r, side)
     return low, high
+
+
+@functools.cache
+def mirror_tables():
+    perm = np.zeros((8, NODES), np.int32)
+    orig = np.full((8, NODES), -1, np.int32)
+    corner = np.zeros((8, CP), np.int32)
+    n = np.arange(NODES)
+    place = [n // (SIDE * ROW), n // ROW % SIDE, n % ROW]
+    real = place[2] < SIDE
+    c = np.arange(CP)
+    for me, bits in enumerate(RELATIVE):
+        x, y, z = [PDEG - q if bit else q for q, bit in zip(place, bits)]
+        perm[me] = np.where(real, (x * SIDE + y) * ROW + z, n)
+        orig[me] = np.where(real, (x * SIDE + y) * SIDE + z, -1)
+        corner[me] = NP * ((c % 8) ^ me) + c // 8
+    return perm, orig, corner
 
 
 @functools.cache
@@ -195,8 +213,30 @@
     return jnp.dot(a, b, preferred_element_type=jnp.float32)
 
 
-def open_kernel(me_ref, beta_ref, y_ref, xl_ref, xh_ref, yl_ref, yh_ref, p_ref, sx_ref, sy_ref):
+def one_hot(mask):
+    return mask.astype(jnp.float32).astype(jnp.bfloat16)
+
+
+def mirror_in(me, perm_ref):
+    row = lax.broadcasted_iota(jnp.int32, (NODES, NODES), 0)
+    return one_hot(row == perm_ref[pl.ds(me, 1), :])
+
+
+def open_kernel(
+    me_ref, proj_ref, wave_ref, perm_ref, orig_ref, corner_ref, xl_ref, xh_ref, yl_ref, yh_ref,
+    beta_ref, y_ref, p_ref, sx_ref, sy_ref, t_ref,
+):
     me = me_ref[0]
+    t_ref[...] = jnp.zeros_like(t_ref)
+    for a in range(SIDE):
+        for b in range(SIDE):
+            t_ref[pl.ds((a * SIDE + b) * ROW, SIDE), :] = wave_ref[a, b].astype(jnp.float32)
+    y_ref[...] = dot(mirror_in(me, perm_ref), t_ref[...].astype(jnp.bfloat16)).astype(jnp.bfloat16)
+    flat = proj_ref[...].reshape(CP, proj_ref.shape[2])
+    spread = one_hot(lax.broadcasted_iota(jnp.int32, (flat.shape[1], NODES), 0) == orig_ref[pl.ds(me, 1), :])
+    order = one_hot(lax.broadcasted_iota(jnp.int32, (CP, CP), 0) == corner_ref[pl.ds(me, 1), :])
+    ordered = dot(order, flat).astype(jnp.bfloat16)
+    beta_ref[...] = dot(ordered, spread).astype(jnp.bfloat16)
     p_ref[...] = dot(beta_ref[...], y_ref[...])
     row = lax.broadcasted_iota(jnp.int32, (NODES, 128), 0)
     zeros = jnp.zeros((FACE, W), jnp.float32)
@@ -213,8 +253,8 @@
             (xl_ref, xh_ref, sx_ref, slot, FACE),
             (yl_ref, yh_ref, sy_ref, (7 - me) ^ r, 0),
         ):
-            low = (row == low_ref[pl.ds(r, 1), :]).astype(jnp.float32).astype(jnp.bfloat16)
-            high = (row == high_ref[pl.ds(r, 1), :]).astype(jnp.float32).astype(jnp.bfloat16)
+            low = one_hot(row == low_ref[pl.ds(r, 1), :])
+            high = one_hot(row == high_ref[pl.ds(r, 1), :])
             packed = dot(beta_ref[pl.ds(0, FACE), :], low) + dot(beta_ref[pl.ds(FACE, FACE), :], high)
             out_ref[to, pl.ds(first, FACE), :] = packed
 
@@ -310,15 +350,19 @@
         put_faces(z_ref, storer(send_ref, me ^ r), r, 1)
 
 
-def close_kernel(me_ref, in_ref, z_ref, mirror_ref, out_ref, t_ref):
+def close_kernel(me_ref, in_ref, z_ref, perm_ref, out_ref, t_ref):
     me = me_ref[0]
     t_ref[...] = z_ref[...]
     for r in range(1, 8):
         add_faces(t_ref, loader(in_ref, me ^ r), r, 1, 0, 0, 0)
-    out_ref[...] = dot(mirror_ref[...], t_ref[...].astype(jnp.bfloat16)).astype(jnp.bfloat16)
-
-
-def call(kernel, me, inputs, outs, scratch=()):
+    y = dot(mirror_in(me, perm_ref), t_ref[...].astype(jnp.bfloat16))
+    for a in range(SIDE):
+        for b in range(SIDE):
+            first = (a * SIDE + b) * ROW
+            out_ref[a, b] = y[first : first + SIDE].astype(jnp.bfloat16)
+
+
+def call(kernel, me, inputs, outs, scratch=(), limit=LIMIT):
     smem = pl.BlockSpec(memory_space=pltpu.SMEM)
     vmem = pl.BlockSpec(memory_space=pltpu.VMEM)
     return pl.pallas_call(
@@ -327,6 +371,7 @@
         in_specs=[smem] + [vmem] * len(inputs),
         out_specs=[vmem] * len(outs),
         scratch_shapes=[pltpu.VMEM(shape, dtype) for shape, dtype in scratch],
+        compiler_params=pltpu.CompilerParams(vmem_limit_bytes=limit),
         interpret=INTERPRET,
     )(me, *inputs)
 
@@ -361,10 +406,6 @@
     back = mirror_of((node_count, NODES), 1)
     ham = exact_dot(into, cell_hamiltonian.reshape(node_count, node_count), ((1,), (0,)))
     ham = exact_dot(ham, back, ((1,), (0,)))
-    betas = mirrored(projectors.reshape(2, 2, 2, NP, node_count), flips).reshape(CP, node_count)
-    betas = exact_dot(betas, back, ((1,), (0,)))
-    current = exact_dot(into, wavefunctions.reshape(node_count, W), ((1,), (0,)))
-
     species = mirrored(atom_species, flips).reshape(8)
     kinds = jnp.arange(1, coupling.shape[0] + 1, dtype=jnp.int32)
     mask = (species[:, None] == kinds).astype(jnp.float32)
@@ -375,11 +416,14 @@
 
     f32, bf16 = jnp.float32, jnp.bfloat16
     (xl, xh), (yl, yh) = lane_tables(1), lane_tables(0)
-    p, sx, sy = call(
+    perm, orig, corner = mirror_tables()
+    by_row = jnp.transpose(projectors.reshape(8, NP, node_count), (1, 0, 2))
+    betas, current, p, sx, sy = call(
         open_kernel,
         me,
-        (betas, current, xl, xh, yl, yh),
-        [((CP, W), f32), ((8, 2 * FACE, W), f32), ((8, FACE, W), f32)],
+        (by_row, wavefunctions, perm, orig, corner, xl, xh, yl, yh),
+        [((CP, NODES), bf16), ((NODES, W), bf16), ((CP, W), f32), ((8, 2 * FACE, W), f32), ((8, FACE, W), f32)],
+        [((NODES, W), f32)],
     )
     ax = swap(sx, 1)
     ay = swap(sy, 0)
@@ -421,8 +465,8 @@
         )
         arrived = swap(send, 1)
         if final:
-            (out,) = call(close_kernel, me, (arrived, z, back), [((node_count, W), bf16)], [(plane, f32)])
-            return out.reshape(wavefunctions.shape)
+            (out,) = call(close_kernel, me, (arrived, z, perm), [(wavefunctions.shape, bf16)], [(plane, f32)])
+            return out
         previous = current
         current, f, send = call(
             vertex_kernel,

time: 239 us -> 213 us (0.89); the launches traced: 234 us -> 211 us
  Pallas kernels: 43.7 us -> 19.9 us
  starting transfers between devices: 23.3 us -> 38.4 us
  blocking collectives: 137 us -> 126 us
  matrix products: 4.37 us -> 1.3 us
  local copies, waits for them, and re-layouts: 9.74 us -> 12.4 us
    pallas_call x12, Pallas kernels: 43.7 us -> 19.9 us  [call(): pl.pallas_call(kernel, out_shape=[jax.ShapeDtypeStruct(shape, dtype) for...]
    all_to_all x3, starting transfers between devices: 23.3 us -> 38.4 us  [swap(): lax.all_to_all(chunks, AXES, 0, 0, axis_index_groups=bricks(sizes, OFFSET...]
    all_to_all x7, blocking collectives: 137 us -> 126 us  [swap(): lax.all_to_all(chunks, AXES, 0, 0, axis_index_groups=bricks(sizes, OFFSET...]
    unnamed x17 -> x55, local copies, waits for them, and re-layouts: 3.72 us -> 11 us
    dot_general x3 -> x1, matrix products: 4.08 us -> 1.01 us  [exact_dot(): lax.dot_general(a, b, (dims, ((), ())), preferred_element_type=jnp.float32)]
    reshape x4 -> x0, local copies, waits for them, and re-layouts: 2.58 us -> none  [the longest x1 1.57 us: local(): return out.reshape(wavefunctions.shape)]
  transfers between devices with their start and end apart: 3 -> 3, of which waited for: 2 -> 2; matrix products, arithmetic and copies ran while one was open for 3% -> 1% of each run, Pallas kernels for 5% -> 4%
where the time goes in v3:
time: 213 us; the launch traced here: 211 us
  blocking collectives  126 us (59%)
  starting transfers between devices  38.4 us (18%)
  Pallas kernels  19.9 us (9%)
  waiting for transfers between devices  12.7 us (6%)
  local copies, waits for them, and re-layouts  12.4 us (6%)
    all_to_all x7, blocking collectives, swap(): lax.all_to_all(chunks, AXES, 0, 0, axis_index_groups=bricks(sizes, OFFSET...  126 us
    all_to_all x3, starting transfers between devices, swap(): lax.all_to_all(chunks, AXES, 0, 0, axis_index_groups=bricks(sizes, OFFSET...  38.4 us
    pallas_call x12, Pallas kernels, call(): pl.pallas_call(kernel, out_shape=[jax.ShapeDtypeStruct(shape, dtype) for...  19.9 us
    all_to_all x3, waiting for transfers between devices, swap(): lax.all_to_all(chunks, AXES, 0, 0, axis_index_groups=bricks(sizes, OFFSET...  12.7 us
    unnamed x55, local copies, waits for them, and re-layouts  11 us
  transfers between devices with their start and end apart: 3, of which 2 were waited for; matrix products, arithmetic and copies ran while one was open for 1% of the time, Pallas kernels for 4%

profile of v3, /device:TPU:1, one launch (start us, length us, event | category | flops | bytes accessed | tf_op | source)
XLA Modules:
  0.0 211.5 jit_solution(10658802167880730172)
XLA Ops:
  2.7 2.1 shard_map.199
  4.7 19.4 %all-to-all-start.1 = ((f32[8,72,128]{2,1,0:T(8,128)}), f32[8,72,128]{2,1,0:T(8,128)S(1)}, u32[]{:S(2)}, u32[]{:S(2)}) async-start(f32[8,72,128]{2,1,0:T(8,128)} %get-tuple-element.36), calls=%async_computation.1 | async-start | bytes 589824 | tf_op jit(solution)/shard_map/all_to_all | solution.py:53
  25.0 3.4 %all-to-all-done.1.in_ref = f32[8,72,128]{2,1,0:T(8,128)S(1)} async-done(((f32[8,72,128]{2,1,0:T(8,128)}), f32[8,72,128]{2,1,0:T(8,128)S(1)}, u32[]{:S(2)}, u32[]{:S(2)}) %all-to-all-start.1) | async-done | bytes 294944 | tf_op jit(solution)/shard_map/all_to_all | solution.py:53
  28.3 7.0 %all-to-all-start = ((f32[8,144,128]{2,1,0:T(8,128)}), f32[8,144,128]{2,1,0:T(8,128)S(1)}, u32[]{:S(2)}, u32[]{:S(2)}) async-start(f32[8,144,128]{2,1,0:T(8,128)} %get-tuple-element.33), calls=%async_computation | async-start | bytes 1179648 | tf_op jit(solution)/shard_map/all_to_all | solution.py:53
  36.3 1.0 convolution_convert_fusion.ham_ref
  37.3 1.0 copy-done.7
  38.4 3.9 %shard_map.200 = (bf16[144,392]{1,0:T(8,128)(2,1)S(1)}, bf16[896,392]{1,0:T(8,128)(2,1)S(1)}) custom-call(s32[1]{0:T(128)} %bitcast.me_ref, f32[8,72,128]{2,1,0:T(8,128)S(1)} %all-to-all-done.1.in_ref, bf16[144,392]{1,0:T(8,128)(2,1)S(1)} %get-tuple-element.37.beta_ref, s32[128,8]{1,0:T(8,128)S(1)} %copy-done.14, s32[128,8]{1,0:T(8,128)S(1)} %copy-done.15, ...), custom_call_target="tpu_custom_call" | custom-call | tf_op jit(solution)/shard_map/pallas_call | solution.py:368
  42.4 9.4 %all-to-all-done.in_ref = f32[8,144,128]{2,1,0:T(8,128)S(1)} async-done(((f32[8,144,128]{2,1,0:T(8,128)}), f32[8,144,128]{2,1,0:T(8,128)S(1)}, u32[]{:S(2)}, u32[]{:S(2)}) %all-to-all-start) | async-done | bytes 589856 | tf_op jit(solution)/shard_map/all_to_all | solution.py:53
  51.8 1.7 shard_map.201
  54.1 12.1 %all-to-all-start.2 = ((f32[8,128,128]{2,1,0:T(8,128)}), f32[8,128,128]{2,1,0:T(8,128)}, u32[]{:S(2)}, u32[]{:S(2)}) async-start(f32[8,128,128]{2,1,0:T(8,128)} %get-tuple-element.39), calls=%async_computation.2 | async-start | bytes 1048576 | tf_op jit(solution)/shard_map/all_to_all | solution.py:53
  68.0 1.0 copy-done.6
  71.4 3.9 %shard_map.202 = (bf16[144,392]{1,0:T(8,128)(2,1)S(1)}, bf16[896,392]{1,0:T(8,128)(2,1)S(1)}) custom-call(s32[1]{0:T(128)} %bitcast.me_ref, f32[8,144,128]{2,1,0:T(8,128)S(1)} %all-to-all-done.in_ref, bf16[144,392]{1,0:T(8,128)(2,1)S(1)} %copy-done.5, s32[128,8]{1,0:T(8,128)S(1)} %copy-done.12, s32[128,8]{1,0:T(8,128)S(1)} %copy-done.13, ...), custom_call_target="tpu_custom_call" | custom-call | tf_op jit(solution)/shard_map/pallas_call | solution.py:368
  76.9 1.9 shard_map.203
  78.8 21.7 %all_to_all.50.in_ref = f32[8,128,128]{2,1,0:T(8,128)S(1)} all-to-all(f32[8,128,128]{2,1,0:T(8,128)S(1)} %get-tuple-element.43), channel_id=1, replica_groups={{128,129,144,145,256,257,272,273},{130,131,146,147,258,259,274,275},{13..., dimensions={0} | all-to-all | bytes 1048576 | tf_op jit(solution)/shard_map/all_to_all | solution.py:53
  100.6 1.1 shard_map.204
  101.7 15.6 %all_to_all.51.in_ref = f32[8,128,128]{2,1,0:T(8,128)S(1)} all-to-all(f32[8,128,128]{2,1,0:T(8,128)S(1)} %get-tuple-element.46), channel_id=1, replica_groups={{17,18,33,34,145,146,161,162},{19,20,35,36,147,148,163,164},{21,22,37,3..., dimensions={0} | all-to-all | bytes 1048576 | tf_op jit(solution)/shard_map/all_to_all | solution.py:53
  118.2 18.4 %all_to_all.52.in_ref = f32[8,128,128]{2,1,0:T(8,128)S(1)} all-to-all(f32[8,128,128]{2,1,0:T(8,128)S(1)} %get-tuple-element.49), channel_id=1, replica_groups={{128,129,144,145,256,257,272,273},{130,131,146,147,258,259,274,275},{13..., dimensions={0} | all-to-all | bytes 1048576 | tf_op jit(solution)/shard_map/all_to_all | solution.py:53
  136.6 1.1 shard_map.206
  137.7 15.6 %all_to_all.53.in_ref = f32[8,128,128]{2,1,0:T(8,128)S(1)} all-to-all(f32[8,128,128]{2,1,0:T(8,128)S(1)} %get-tuple-element.51), channel_id=1, replica_groups={{17,18,33,34,145,146,161,162},{19,20,35,36,147,148,163,164},{21,22,37,3..., dimensions={0} | all-to-all | bytes 1048576 | tf_op jit(solution)/shard_map/all_to_all | solution.py:53
  154.2 24.3 %all_to_all.54.in_ref = f32[8,128,128]{2,1,0:T(8,128)S(1)} all-to-all(f32[8,128,128]{2,1,0:T(8,128)S(1)} %get-tuple-element.54), channel_id=1, replica_groups={{128,129,144,145,256,257,272,273},{130,131,146,147,258,259,274,275},{13..., dimensions={0} | all-to-all | bytes 1048576 | tf_op jit(solution)/shard_map/all_to_all | solution.py:53
  178.4 1.1 shard_map.208
  179.5 15.6 %all_to_all.55.in_ref = f32[8,128,128]{2,1,0:T(8,128)S(1)} all-to-all(f32[8,128,128]{2,1,0:T(8,128)S(1)} %get-tuple-element.56), channel_id=1, replica_groups={{17,18,33,34,145,146,161,162},{19,20,35,36,147,148,163,164},{21,22,37,3..., dimensions={0} | all-to-all | bytes 1048576 | tf_op jit(solution)/shard_map/all_to_all | solution.py:53
  195.7 14.8 %all_to_all.56.in_ref = f32[8,56,128]{2,1,0:T(8,128)S(1)} all-to-all(f32[8,56,128]{2,1,0:T(8,128)S(1)} %get-tuple-element.59), channel_id=1, replica_groups={{128,129,144,145,256,257,272,273},{130,131,146,147,258,259,274,275},{13..., dimensions={0} | all-to-all | bytes 458752 | tf_op jit(solution)/shard_map/all_to_all | solution.py:53
  210.5 1.0 shard_map.210
  (78 shorter events, 13.0 us)
Async XLA Ops:
  0.0 36.2 %copy-start = (bf16[1,1,1,343,343]{4,3,2,1,0:T(8,128)(2,1)S(1)}, bf16[1,1,1,343,343]{4,3,2,1,0:T(8,128)(2,1)}, u32[]{:S(2)}) copy-start(bf16[1,1,1,343,343]{4,3,2,1,0:T(8,128)(2,1)} %param.22) | copy-start | bytes 705898
  0.0 0.8 copy-start.22
  0.0 0.8 copy-start.21
  0.0 0.8 copy-start.20
  0.1 0.8 copy-start.16
  0.1 0.8 copy-start.19
  0.9 0.9 copy-start.10
  1.8 0.9 copy-start.11
  4.7 32.6 %copy-start.4 = (bf16[144,392]{1,0:T(8,128)(2,1)}, bf16[144,392]{1,0:T(8,128)(2,1)S(1)}, u32[]{:S(2)}) copy-start(bf16[144,392]{1,0:T(8,128)(2,1)S(1)} %get-tuple-element.37.beta_ref) | copy-start | bytes 338692
  4.7 23.6 %all-to-all-start.1 = ((f32[8,72,128]{2,1,0:T(8,128)}), f32[8,72,128]{2,1,0:T(8,128)S(1)}, u32[]{:S(2)}, u32[]{:S(2)}) async-start(f32[8,72,128]{2,1,0:T(8,128)} %get-tuple-element.36), calls=%async_computation.1 | async-start | bytes 589824 | tf_op jit(solution)/shard_map/all_to_all | solution.py:53
  28.3 7.1 %copy-start.25 = (f32[2,18,18]{2,0,1:T(2,128)S(1)}, f32[2,18,18]{2,0,1:T(2,128)}, u32[]{:S(2)}) copy-start(f32[2,18,18]{2,0,1:T(2,128)} %param.25) | copy-start | bytes 7780
  28.3 23.5 %all-to-all-start = ((f32[8,144,128]{2,1,0:T(8,128)}), f32[8,144,128]{2,1,0:T(8,128)S(1)}, u32[]{:S(2)}, u32[]{:S(2)}) async-start(f32[8,144,128]{2,1,0:T(8,128)} %get-tuple-element.33), calls=%async_computation | async-start | bytes 1179648 | tf_op jit(solution)/shard_map/all_to_all | solution.py:53
  36.2 1.1 copy-start.14
  36.2 1.1 copy-start.15
  36.2 1.1 copy-start.18
  37.3 1.0 copy-start.7
  54.1 21.8 %all-to-all-start.2 = ((f32[8,128,128]{2,1,0:T(8,128)}), f32[8,128,128]{2,1,0:T(8,128)}, u32[]{:S(2)}, u32[]{:S(2)}) async-start(f32[8,128,128]{2,1,0:T(8,128)} %get-tuple-element.39), calls=%async_computation.2 | async-start | bytes 1048576 | tf_op jit(solution)/shard_map/all_to_all | solution.py:53
  67.0 0.9 copy-start.5
  68.0 1.0 copy-start.6
  69.0 0.8 copy-start.12
  69.8 0.8 copy-start.13
  71.4 4.6 %copy-start.1 = (f32[392,1]{1,0:T(8,128)S(1)}, f32[392,1]{1,0:T(8,128)}, u32[]{:S(2)}) copy-start(f32[392,1]{1,0:T(8,128)} %constant.171.clone.share_ref) | copy-start | bytes 4708
  76.0 0.9 copy-start.9
  78.8 21.7 %copy-start.3 = (bf16[144,392]{1,0:T(8,128)(2,1)S(1)}, bf16[144,392]{1,0:T(8,128)(2,1)}, u32[]{:S(2)}) copy-start(bf16[144,392]{1,0:T(8,128)(2,1)} %copy-done.2) | copy-start | bytes 338692
  (6 other events, 4.2 us)

commit v4 on v3

--- a/solution.py
+++ b/solution.py
@@ -26,6 +26,8 @@
 FACE = 72
 EDGE = 112
 LAST = 127
+FAR = 7 * CHUNK
+ROWS = FAR + CP
 LIMIT = 12 << 20
 
 AXES = ("gx", "gy", "gz")
@@ -120,12 +122,12 @@
         perm[me] = np.where(real, (x * SIDE + y) * ROW + z, n)
         orig[me] = np.where(real, (x * SIDE + y) * SIDE + z, -1)
         corner[me] = NP * ((c % 8) ^ me) + c // 8
-    return perm, orig, corner
+    return np.concatenate([perm, orig]), corner
 
 
 @functools.cache
 def corner_table(side):
-    table = np.full((CP + 7 * CHUNK, 8), -1, np.int32)
+    table = np.full((ROWS, 8), -1, np.int32)
 
     def fill(first, lattice):
         for s, bits in enumerate(RELATIVE):
@@ -135,20 +137,12 @@
                 table[first : first + NP, s] = NP * v + np.arange(NP)
 
     for v, e in enumerate(RELATIVE):
-        fill(NP * v, e)
+        fill(FAR + NP * v, e)
     for r in range(1, 8):
         for k, v in enumerate(near(r, side)):
             lattice = [2 * side - e if bit else e for e, bit in zip(RELATIVE[v], RELATIVE[r])]
-            fill(CP + (r - 1) * CHUNK + NP * k, lattice)
-    return table
-
-
-def node_masks(side):
-    masks = np.ones((8, NODES), np.float32)
-    for r in range(1, 8):
-        nodes = face_nodes(r, side)
-        masks[r, nodes[nodes >= 0]] = 0.0
-    return masks
+            fill((r - 1) * CHUNK + NP * k, lattice)
+    return table.T
 
 
 def add_faces(ref, part, r, side, face=FACE, edge=EDGE, last=LAST):
@@ -223,8 +217,7 @@
 
 
 def open_kernel(
-    me_ref, proj_ref, wave_ref, perm_ref, orig_ref, corner_ref, xl_ref, xh_ref, yl_ref, yh_ref,
-    beta_ref, y_ref, p_ref, sx_ref, sy_ref, t_ref,
+    me_ref, proj_ref, wave_ref, perm_ref, corner_ref, lane_ref, beta_ref, turned_ref, y_ref, p_ref, sx_ref, sy_ref, t_ref
 ):
     me = me_ref[0]
     t_ref[...] = jnp.zeros_like(t_ref)
@@ -233,11 +226,13 @@
             t_ref[pl.ds((a * SIDE + b) * ROW, SIDE), :] = wave_ref[a, b].astype(jnp.float32)
     y_ref[...] = dot(mirror_in(me, perm_ref), t_ref[...].astype(jnp.bfloat16)).astype(jnp.bfloat16)
     flat = proj_ref[...].reshape(CP, proj_ref.shape[2])
-    spread = one_hot(lax.broadcasted_iota(jnp.int32, (flat.shape[1], NODES), 0) == orig_ref[pl.ds(me, 1), :])
+    spread = one_hot(lax.broadcasted_iota(jnp.int32, (flat.shape[1], NODES), 0) == perm_ref[pl.ds(8 + me, 1), :])
     order = one_hot(lax.broadcasted_iota(jnp.int32, (CP, CP), 0) == corner_ref[pl.ds(me, 1), :])
     ordered = dot(order, flat).astype(jnp.bfloat16)
     beta_ref[...] = dot(ordered, spread).astype(jnp.bfloat16)
     p_ref[...] = dot(beta_ref[...], y_ref[...])
+    same = one_hot(lax.broadcasted_iota(jnp.int32, (NODES, NODES), 0) == lax.broadcasted_iota(jnp.int32, (NODES, NODES), 1))
+    turned_ref[...] = dot_nt(same, beta_ref[...]).astype(jnp.bfloat16)
     row = lax.broadcasted_iota(jnp.int32, (NODES, 128), 0)
     zeros = jnp.zeros((FACE, W), jnp.float32)
     sx_ref[me] = jnp.zeros((2 * FACE, W), jnp.float32)
@@ -249,35 +244,64 @@
         used = NP * len(shared(r, 1))
         if used < FACE:
             sx_ref[slot, pl.ds(used, FACE - used), :] = jnp.zeros((FACE - used, W), jnp.float32)
-        for low_ref, high_ref, out_ref, to, first in (
-            (xl_ref, xh_ref, sx_ref, slot, FACE),
-            (yl_ref, yh_ref, sy_ref, (7 - me) ^ r, 0),
-        ):
-            low = one_hot(row == low_ref[pl.ds(r, 1), :])
-            high = one_hot(row == high_ref[pl.ds(r, 1), :])
+        for base, out_ref, to, first in ((0, sx_ref, slot, FACE), (16, sy_ref, (7 - me) ^ r, 0)):
+            low = one_hot(row == lane_ref[pl.ds(base + r, 1), :])
+            high = one_hot(row == lane_ref[pl.ds(base + 8 + r, 1), :])
             packed = dot(beta_ref[pl.ds(0, FACE), :], low) + dot(beta_ref[pl.ds(FACE, FACE), :], high)
             out_ref[to, pl.ds(first, FACE), :] = packed
 
 
-def assemble_kernel(first, flip, me_ref, in_ref, beta_ref, low_ref, high_ref, table_ref, mask_ref, own_ref, far_ref, acc_ref):
-    me = me_ref[0] ^ flip
-    lane = lax.broadcasted_iota(jnp.int32, (128, NODES), 1)
-    pick = lax.broadcasted_iota(jnp.int32, (CP + 7 * CHUNK, CP), 1)
-
-    def chosen(s):
-        return (pick == table_ref[:, pl.ds(s, 1)]).astype(jnp.float32).astype(jnp.bfloat16)
-
-    acc_ref[...] = dot(chosen(0), beta_ref[...])
+def dot_nt(a, b):
+    if INTERPRET:
+        a, b = a.astype(jnp.float32), b.astype(jnp.float32)
+    return lax.dot_general(a, b, (((1,), (1,)), ((), ())), preferred_element_type=jnp.float32)
+
+
+def dot_tn(a, b):
+    if INTERPRET:
+        a, b = a.astype(jnp.float32), b.astype(jnp.float32)
+    return lax.dot_general(a, b, (((0,), (0,)), ((), ())), preferred_element_type=jnp.float32)
+
+
+def assemble_kernel(side, first, me_ref, in_ref, beta_ref, lane_ref, table_ref, own_ref, far_ref, acc_ref):
+    me = me_ref[0] if side else 7 - me_ref[0]
+    base = 16 * (1 - side)
+    node = lax.broadcasted_iota(jnp.int32, (NODES, 128), 0)
+
+    def chosen(s, at, rows):
+        pick = lax.broadcasted_iota(jnp.int32, (rows, ROWS), 0) + at
+        return one_hot(pick == table_ref[pl.ds(8 * (1 - side) + s, 1), :])
+
+    if side:
+        acc_ref[...] = dot_tn(chosen(0, 0, CP), beta_ref[...])
+    else:
+        acc_ref[...] = dot(beta_ref[...], chosen(0, 0, CP))
     for s in range(1, 8):
         packed = in_ref[me ^ s, pl.ds(first, FACE), :].astype(jnp.bfloat16)
-        low = (lane == low_ref[:, pl.ds(s, 1)]).astype(jnp.float32).astype(jnp.bfloat16)
-        high = (lane == high_ref[:, pl.ds(s, 1)]).astype(jnp.float32).astype(jnp.bfloat16)
-        spread = jnp.concatenate([dot(packed, low), dot(packed, high)], axis=0).astype(jnp.bfloat16)
-        acc_ref[...] = acc_ref[...] + dot(chosen(s), spread)
-    own_ref[...] = acc_ref[pl.ds(0, CP), :].astype(jnp.bfloat16)
-    for r in range(1, 8):
-        block = acc_ref[pl.ds(CP + (r - 1) * CHUNK, CHUNK), :] * mask_ref[pl.ds(r, 1), :]
-        far_ref[pl.ds((r - 1) * CHUNK, CHUNK), :] = block.astype(jnp.bfloat16)
+        for half in range(2):
+            spread = one_hot(node == lane_ref[pl.ds(base + 8 * half + s, 1), :])
+            pick = chosen(s, FACE * half, FACE)
+            if side:
+                term = dot_tn(pick, dot_nt(packed, spread).astype(jnp.bfloat16))
+            else:
+                term = dot(dot_nt(spread, packed).astype(jnp.bfloat16), pick)
+            acc_ref[...] = acc_ref[...] + term
+    for r in range(1, 8):
+        touched = (node == lane_ref[pl.ds(base + r, 1), :]).astype(jnp.float32)
+        if side:
+            mask = 1.0 - lax.dot_general(
+                jnp.ones((8, 128), jnp.float32), touched, (((1,), (1,)), ((), ())), preferred_element_type=jnp.float32
+            )
+            block = acc_ref[pl.ds((r - 1) * CHUNK, CHUNK), :] * mask[0:1, :]
+            far_ref[pl.ds((r - 1) * CHUNK, CHUNK), :] = block.astype(jnp.bfloat16)
+        else:
+            mask = 1.0 - jnp.sum(touched, axis=1, keepdims=True)
+            block = acc_ref[:, pl.ds((r - 1) * CHUNK, CHUNK)] * mask
+            far_ref[:, pl.ds((r - 1) * CHUNK, CHUNK)] = block.astype(jnp.bfloat16)
+    if side:
+        own_ref[...] = acc_ref[pl.ds(FAR, CP), :].astype(jnp.bfloat16)
+    else:
+        own_ref[...] = acc_ref[:, pl.ds(FAR, CP)].astype(jnp.bfloat16)
 
 
 def send_terms(me, corr_ref, coupling_ref, ham_ref, y, own_ref, c_ref, f_ref, send_ref):
@@ -415,39 +439,48 @@
     blocks = jnp.where(corner_of[:, None] == corner_of[None, :], blocks, 0.0)
 
     f32, bf16 = jnp.float32, jnp.bfloat16
-    (xl, xh), (yl, yh) = lane_tables(1), lane_tables(0)
-    perm, orig, corner = mirror_tables()
+    lanes = np.concatenate([*lane_tables(1), *lane_tables(0)])
+    tables = np.concatenate([corner_table(1), corner_table(0)])
+    perm, corner = mirror_tables()
     by_row = jnp.transpose(projectors.reshape(8, NP, node_count), (1, 0, 2))
-    betas, current, p, sx, sy = call(
+    plane = (NODES, W)
+    betas, turned, current, p, sx, sy = call(
         open_kernel,
         me,
-        (by_row, wavefunctions, perm, orig, corner, xl, xh, yl, yh),
-        [((CP, NODES), bf16), ((NODES, W), bf16), ((CP, W), f32), ((8, 2 * FACE, W), f32), ((8, FACE, W), f32)],
-        [((NODES, W), f32)],
+        (by_row, wavefunctions, perm, corner, lanes),
+        [
+            ((CP, NODES), bf16),
+            ((NODES, CP), bf16),
+            (plane, bf16),
+            ((CP, W), f32),
+            ((8, 2 * FACE, W), f32),
+            ((8, FACE, W), f32),
+        ],
+        [(plane, f32)],
+        58 << 20,
     )
     ax = swap(sx, 1)
     ay = swap(sy, 0)
-
-    def assemble(side, arrived, first):
-        low, high = lane_tables(side)
-        return call(
-            functools.partial(assemble_kernel, first, 0 if side else 7),
-            me,
-            (arrived, betas, low.T.copy(), high.T.copy(), corner_table(side), node_masks(side)),
-            [((CP, NODES), bf16), ((7 * CHUNK, NODES), bf16)],
-            [((CP + 7 * CHUNK, NODES), f32)],
-        )
-
-    ownx, farx = assemble(1, ax, FACE)
-    owny, fary = assemble(0, ay, 0)
-    owny, fary = owny.T, fary.T
+    ownx, farx = call(
+        functools.partial(assemble_kernel, 1, FACE),
+        me,
+        (ax, betas, lanes, tables),
+        [((CP, NODES), bf16), ((FAR, NODES), bf16)],
+        [((ROWS, NODES), f32)],
+    )
+    owny, fary = call(
+        functools.partial(assemble_kernel, 0, 0),
+        me,
+        (ay, turned, lanes, tables),
+        [((NODES, CP), bf16), ((NODES, FAR), bf16)],
+        [((NODES, ROWS), f32)],
+    )
 
     node = np.arange(NODES)
     place = [node // (SIDE * ROW), (node // ROW) % SIDE, node % ROW]
     share = np.prod([np.where(q == PDEG, 0.5, 1.0) for q in place], axis=0).astype(np.float32).reshape(NODES, 1)
 
     packet = ((8, CHUNK, W), f32)
-    plane = (NODES, W)
     f, send = call(
         first_kernel, me, (ax, p, current, blocks, ham, owny), [(plane, f32), packet], [((CP, W), f32)] * 2
     )

time: 213 us -> 213 us (level)
  local copies, waits for them, and re-layouts: 12.4 us -> 5.33 us
  Pallas kernels: 19.9 us -> 25.4 us
  blocking collectives: 126 us -> 129 us
    unnamed x55 -> x33, local copies, waits for them, and re-layouts: 11 us -> 4.9 us
    pallas_call x12, Pallas kernels: 19.9 us -> 25.4 us  [call(): pl.pallas_call(kernel, out_shape=[jax.ShapeDtypeStruct(shape, dtype) for...]
    all_to_all x7, blocking collectives: 126 us -> 129 us  [swap(): lax.all_to_all(chunks, AXES, 0, 0, axis_index_groups=bricks(sizes, OFFSET...]
  transfers between devices with their start and end apart: 3 -> 3, of which waited for: 2 -> 2; matrix products, arithmetic and copies ran while one was open for 1% -> 1% of each run, Pallas kernels for 4% -> 6%
where the time goes in v4:
time: 213 us; the launch traced here: 212 us
  blocking collectives  129 us (61%)
  starting transfers between devices  38.4 us (18%)
  Pallas kernels  25.4 us (12%)
  waiting for transfers between devices  12.4 us (6%)
  local copies, waits for them, and re-layouts  5.33 us (3%)
    all_to_all x7, blocking collectives, swap(): lax.all_to_all(chunks, AXES, 0, 0, axis_index_groups=bricks(sizes, OFFSET...  129 us
    all_to_all x3, starting transfers between devices, swap(): lax.all_to_all(chunks, AXES, 0, 0, axis_index_groups=bricks(sizes, OFFSET...  38.4 us
    pallas_call x12, Pallas kernels, call(): pl.pallas_call(kernel, out_shape=[jax.ShapeDtypeStruct(shape, dtype) for...  25.4 us
    all_to_all x3, waiting for transfers between devices, swap(): lax.all_to_all(chunks, AXES, 0, 0, axis_index_groups=bricks(sizes, OFFSET...  12.4 us
    unnamed x33, local copies, waits for them, and re-layouts  4.9 us
  transfers between devices with their start and end apart: 3, of which 2 were waited for; matrix products, arithmetic and copies ran while one was open for 1% of the time, Pallas kernels for 6%

profile of v4, /device:TPU:1, one launch (start us, length us, event | category | flops | bytes accessed | tf_op | source)
XLA Modules:
  0.0 212.3 jit_solution(8388712842197745447)
XLA Ops:
  0.0 3.2 %shard_map.100 = (bf16[144,392]{1,0:T(8,128)(2,1)}, bf16[392,144]{1,0:T(8,128)(2,1)}, bf16[392,128]{1,0:T(8,128)(2,1)}, f32[144,128]{1,0:T(8,128)}, f32[8,144,128]{2,1,0:T(8,128)}, /*index=5*/f32[8,72,128]{2,1,0:T(8,128)}) custom-call(s32[1]{0:T(128)} %bitcast.me_ref, bf16[18,8,343]{2,1,0:T(8,128)(2,1)} %bitcast.16, bf16[7,7,7,128]{3,2,1,0:T(8,128)(2,1)} %wave_ref.1, ...), custom_call_target="tpu_custom_call" | custom-call | tf_op jit(solution)/shard_map/pallas_call | solution.py:392
  3.2 19.4 %all-to-all-start.1 = ((f32[8,72,128]{2,1,0:T(8,128)}), f32[8,72,128]{2,1,0:T(8,128)S(1)}, u32[]{:S(2)}, u32[]{:S(2)}) async-start(f32[8,72,128]{2,1,0:T(8,128)} %get-tuple-element.37), calls=%async_computation.1 | async-start | bytes 589824 | tf_op jit(solution)/shard_map/all_to_all | solution.py:55
  23.4 3.4 %all-to-all-done.1.in_ref = f32[8,72,128]{2,1,0:T(8,128)S(1)} async-done(((f32[8,72,128]{2,1,0:T(8,128)}), f32[8,72,128]{2,1,0:T(8,128)S(1)}, u32[]{:S(2)}, u32[]{:S(2)}) %all-to-all-start.1) | async-done | bytes 294944 | tf_op jit(solution)/shard_map/all_to_all | solution.py:55
  26.8 7.0 %all-to-all-start = ((f32[8,144,128]{2,1,0:T(8,128)}), f32[8,144,128]{2,1,0:T(8,128)S(1)}, u32[]{:S(2)}, u32[]{:S(2)}) async-start(f32[8,144,128]{2,1,0:T(8,128)} %get-tuple-element.34), calls=%async_computation | async-start | bytes 1179648 | tf_op jit(solution)/shard_map/all_to_all | solution.py:55
  34.7 1.0 convolution_convert_fusion.ham_ref
  35.8 5.5 %shard_map.101 = (bf16[392,144]{1,0:T(8,128)(2,1)S(1)}, bf16[392,896]{1,0:T(8,128)(2,1)S(1)}) custom-call(s32[1]{0:T(128)} %bitcast.me_ref, f32[8,72,128]{2,1,0:T(8,128)S(1)} %all-to-all-done.1.in_ref, bf16[392,144]{1,0:T(8,128)(2,1)S(1)} %copy-done.7, s32[32,128]{1,0:T(8,128)S(1)} %copy-done.10, s32[16,1040]{1,0:T(8,128)S(1)} %copy-done.5), custom_call_target="tpu_custom_call" | custom-call | tf_op jit(solution)/shard_map/pallas_call | solution.py:392
  41.2 9.0 %all-to-all-done.in_ref = f32[8,144,128]{2,1,0:T(8,128)S(1)} async-done(((f32[8,144,128]{2,1,0:T(8,128)}), f32[8,144,128]{2,1,0:T(8,128)S(1)}, u32[]{:S(2)}, u32[]{:S(2)}) %all-to-all-start) | async-done | bytes 589856 | tf_op jit(solution)/shard_map/all_to_all | solution.py:55
  50.2 1.7 shard_map.102
  52.6 12.1 %all-to-all-start.2 = ((f32[8,128,128]{2,1,0:T(8,128)}), f32[8,128,128]{2,1,0:T(8,128)}, u32[]{:S(2)}, u32[]{:S(2)}) async-start(f32[8,128,128]{2,1,0:T(8,128)} %get-tuple-element.40), calls=%async_computation.2 | async-start | bytes 1048576 | tf_op jit(solution)/shard_map/all_to_all | solution.py:55
  65.6 0.9 copy-done.11
  66.5 6.7 %shard_map.103 = (bf16[144,392]{1,0:T(8,128)(2,1)S(1)}, bf16[896,392]{1,0:T(8,128)(2,1)S(1)}) custom-call(s32[1]{0:T(128)} %bitcast.me_ref, f32[8,144,128]{2,1,0:T(8,128)S(1)} %all-to-all-done.in_ref, bf16[144,392]{1,0:T(8,128)(2,1)S(1)} %copy-done.11, s32[32,128]{1,0:T(8,128)S(1)} %copy-done.10, s32[16,1040]{1,0:T(8,128)S(1)} %copy-done.6), custom_call_target="tpu_custom_call" | custom-call | tf_op jit(solution)/shard_map/pallas_call | solution.py:392
  73.9 0.9 copy-done.9
  74.8 1.9 shard_map.104
  76.7 20.9 %all_to_all.50.in_ref = f32[8,128,128]{2,1,0:T(8,128)S(1)} all-to-all(f32[8,128,128]{2,1,0:T(8,128)S(1)} %get-tuple-element.45), channel_id=1, replica_groups={{128,129,144,145,256,257,272,273},{130,131,146,147,258,259,274,275},{13..., dimensions={0} | all-to-all | bytes 1048576 | tf_op jit(solution)/shard_map/all_to_all | solution.py:55
  97.6 1.1 shard_map.105
  98.7 15.6 %all_to_all.51.in_ref = f32[8,128,128]{2,1,0:T(8,128)S(1)} all-to-all(f32[8,128,128]{2,1,0:T(8,128)S(1)} %get-tuple-element.48), channel_id=1, replica_groups={{17,18,33,34,145,146,161,162},{19,20,35,36,147,148,163,164},{21,22,37,3..., dimensions={0} | all-to-all | bytes 1048576 | tf_op jit(solution)/shard_map/all_to_all | solution.py:55
  115.2 19.8 %all_to_all.52.in_ref = f32[8,128,128]{2,1,0:T(8,128)S(1)} all-to-all(f32[8,128,128]{2,1,0:T(8,128)S(1)} %get-tuple-element.51), channel_id=1, replica_groups={{128,129,144,145,256,257,272,273},{130,131,146,147,258,259,274,275},{13..., dimensions={0} | all-to-all | bytes 1048576 | tf_op jit(solution)/shard_map/all_to_all | solution.py:55
  135.0 1.1 shard_map.107
  136.1 15.6 %all_to_all.53.in_ref = f32[8,128,128]{2,1,0:T(8,128)S(1)} all-to-all(f32[8,128,128]{2,1,0:T(8,128)S(1)} %get-tuple-element.53), channel_id=1, replica_groups={{17,18,33,34,145,146,161,162},{19,20,35,36,147,148,163,164},{21,22,37,3..., dimensions={0} | all-to-all | bytes 1048576 | tf_op jit(solution)/shard_map/all_to_all | solution.py:55
  152.6 22.4 %all_to_all.54.in_ref = f32[8,128,128]{2,1,0:T(8,128)S(1)} all-to-all(f32[8,128,128]{2,1,0:T(8,128)S(1)} %get-tuple-element.56), channel_id=1, replica_groups={{128,129,144,145,256,257,272,273},{130,131,146,147,258,259,274,275},{13..., dimensions={0} | all-to-all | bytes 1048576 | tf_op jit(solution)/shard_map/all_to_all | solution.py:55
  175.0 1.1 shard_map.109
  176.1 16.7 %all_to_all.55.in_ref = f32[8,128,128]{2,1,0:T(8,128)S(1)} all-to-all(f32[8,128,128]{2,1,0:T(8,128)S(1)} %get-tuple-element.58), channel_id=1, replica_groups={{17,18,33,34,145,146,161,162},{19,20,35,36,147,148,163,164},{21,22,37,3..., dimensions={0} | all-to-all | bytes 1048576 | tf_op jit(solution)/shard_map/all_to_all | solution.py:55
  193.3 18.0 %all_to_all.56.in_ref = f32[8,56,128]{2,1,0:T(8,128)S(1)} all-to-all(f32[8,56,128]{2,1,0:T(8,128)S(1)} %get-tuple-element.61), channel_id=1, replica_groups={{128,129,144,145,256,257,272,273},{130,131,146,147,258,259,274,275},{13..., dimensions={0} | all-to-all | bytes 458752 | tf_op jit(solution)/shard_map/all_to_all | solution.py:55
  211.4 1.0 shard_map.111
  (54 shorter events, 6.2 us)
Async XLA Ops:
  0.0 34.7 %copy-start = (bf16[1,1,1,343,343]{4,3,2,1,0:T(8,128)(2,1)S(1)}, bf16[1,1,1,343,343]{4,3,2,1,0:T(8,128)(2,1)}, u32[]{:S(2)}) copy-start(bf16[1,1,1,343,343]{4,3,2,1,0:T(8,128)(2,1)} %param.11) | copy-start | bytes 705898
  3.2 23.6 %all-to-all-start.1 = ((f32[8,72,128]{2,1,0:T(8,128)}), f32[8,72,128]{2,1,0:T(8,128)S(1)}, u32[]{:S(2)}, u32[]{:S(2)}) async-start(f32[8,72,128]{2,1,0:T(8,128)} %get-tuple-element.37), calls=%async_computation.1 | async-start | bytes 589824 | tf_op jit(solution)/shard_map/all_to_all | solution.py:55
  22.6 0.7 copy-start.15
  26.8 7.1 %copy-start.14 = (f32[2,18,18]{2,0,1:T(2,128)S(1)}, f32[2,18,18]{2,0,1:T(2,128)}, u32[]{:S(2)}) copy-start(f32[2,18,18]{2,0,1:T(2,128)} %param.14) | copy-start | bytes 7780
  26.8 23.5 %all-to-all-start = ((f32[8,144,128]{2,1,0:T(8,128)}), f32[8,144,128]{2,1,0:T(8,128)S(1)}, u32[]{:S(2)}, u32[]{:S(2)}) async-start(f32[8,144,128]{2,1,0:T(8,128)} %get-tuple-element.34), calls=%async_computation | async-start | bytes 1179648 | tf_op jit(solution)/shard_map/all_to_all | solution.py:55
  34.7 1.1 copy-start.5
  34.7 1.1 copy-start.7
  34.7 1.1 copy-start.10
  35.8 14.5 %copy-start.2 = (bf16[392,128]{1,0:T(8,128)(2,1)S(1)}, bf16[392,128]{1,0:T(8,128)(2,1)}, u32[]{:S(2)}) copy-start(bf16[392,128]{1,0:T(8,128)(2,1)} %get-tuple-element.36.y_ref.before_ref) | copy-start | bytes 301060
  35.8 14.5 %copy-start.13 = (f32[144,128]{1,0:T(8,128)S(1)}, f32[144,128]{1,0:T(8,128)}, u32[]{:S(2)}) copy-start(f32[144,128]{1,0:T(8,128)} %get-tuple-element.35.p_ref) | copy-start | bytes 221188
  51.9 0.7 copy-start.8
  52.6 21.3 %all-to-all-start.2 = ((f32[8,128,128]{2,1,0:T(8,128)}), f32[8,128,128]{2,1,0:T(8,128)}, u32[]{:S(2)}, u32[]{:S(2)}) async-start(f32[8,128,128]{2,1,0:T(8,128)} %get-tuple-element.40), calls=%async_computation.2 | async-start | bytes 1048576 | tf_op jit(solution)/shard_map/all_to_all | solution.py:55
  64.7 0.9 copy-start.6
  65.6 0.9 copy-start.11
  66.5 7.4 %copy-start.1 = (f32[392,1]{1,0:T(8,128)S(1)}, f32[392,1]{1,0:T(8,128)}, u32[]{:S(2)}) copy-start(f32[392,1]{1,0:T(8,128)} %constant.138.clone.share_ref) | copy-start | bytes 4708
  73.2 0.7 copy-start.3
  73.9 0.9 copy-start.9
  76.7 20.9 %copy-start.4 = (bf16[144,392]{1,0:T(8,128)(2,1)S(1)}, bf16[144,392]{1,0:T(8,128)(2,1)}, u32[]{:S(2)}) copy-start(bf16[144,392]{1,0:T(8,128)(2,1)} %copy-done.3) | copy-start | bytes 338692
  193.3 18.0 %copy-start.12 = (s32[16,392]{1,0:T(8,128)S(1)}, s32[16,392]{1,0:T(8,128)}, u32[]{:S(2)}) copy-start(s32[16,392]{1,0:T(8,128)} %constant.134.clone.perm_ref) | copy-start | bytes 75268

commit v5 on v4

--- a/solution.py
+++ b/solution.py
@@ -263,45 +263,50 @@
     return lax.dot_general(a, b, (((0,), (0,)), ((), ())), preferred_element_type=jnp.float32)
 
 
-def assemble_kernel(side, first, me_ref, in_ref, beta_ref, lane_ref, table_ref, own_ref, far_ref, acc_ref):
-    me = me_ref[0] if side else 7 - me_ref[0]
-    base = 16 * (1 - side)
+def chosen(table_ref, s, at, rows):
+    pick = lax.broadcasted_iota(jnp.int32, (rows, ROWS), 0) + at
+    return one_hot(pick == table_ref[pl.ds(s, 1), :])
+
+
+def assemble_rows_kernel(
+    first, me_ref, in_ref, beta_ref, lane_ref, table_ref, own_ref, far_ref, acc_ref, pick_ref, spread_ref
+):
+    me = me_ref[0]
     node = lax.broadcasted_iota(jnp.int32, (NODES, 128), 0)
-
-    def chosen(s, at, rows):
-        pick = lax.broadcasted_iota(jnp.int32, (rows, ROWS), 0) + at
-        return one_hot(pick == table_ref[pl.ds(8 * (1 - side) + s, 1), :])
-
-    if side:
-        acc_ref[...] = dot_tn(chosen(0, 0, CP), beta_ref[...])
-    else:
-        acc_ref[...] = dot(beta_ref[...], chosen(0, 0, CP))
+    pick_ref[pl.ds(0, CP), :] = chosen(table_ref, 0, 0, CP)
+    spread_ref[pl.ds(0, CP), :] = beta_ref[...].astype(jnp.float32)
+    for s in range(1, 8):
+        pick_ref[pl.ds(CP * s, CP), :] = chosen(table_ref, s, 0, CP)
+        packed = in_ref[me ^ s, pl.ds(first, FACE), :].astype(jnp.bfloat16)
+        for half in range(2):
+            spread = one_hot(node == lane_ref[pl.ds(8 * half + s, 1), :])
+            spread_ref[pl.ds(CP * s + FACE * half, FACE), :] = dot_nt(packed, spread)
+    acc_ref[...] = dot_tn(pick_ref[...], spread_ref[...].astype(jnp.bfloat16))
+    for r in range(1, 8):
+        touched = (node == lane_ref[pl.ds(r, 1), :]).astype(jnp.float32)
+        mask = 1.0 - lax.dot_general(
+            jnp.ones((8, 128), jnp.float32), touched, (((1,), (1,)), ((), ())), preferred_element_type=jnp.float32
+        )
+        block = acc_ref[pl.ds((r - 1) * CHUNK, CHUNK), :] * mask[0:1, :]
+        far_ref[pl.ds((r - 1) * CHUNK, CHUNK), :] = block.astype(jnp.bfloat16)
+    own_ref[...] = acc_ref[pl.ds(FAR, CP), :].astype(jnp.bfloat16)
+
+
+def assemble_columns_kernel(first, me_ref, in_ref, beta_ref, lane_ref, table_ref, own_ref, far_ref, acc_ref):
+    me = 7 - me_ref[0]
+    node = lax.broadcasted_iota(jnp.int32, (NODES, 128), 0)
+    acc_ref[...] = dot(beta_ref[...], chosen(table_ref, 8, 0, CP))
     for s in range(1, 8):
         packed = in_ref[me ^ s, pl.ds(first, FACE), :].astype(jnp.bfloat16)
         for half in range(2):
-            spread = one_hot(node == lane_ref[pl.ds(base + 8 * half + s, 1), :])
-            pick = chosen(s, FACE * half, FACE)
-            if side:
-                term = dot_tn(pick, dot_nt(packed, spread).astype(jnp.bfloat16))
-            else:
-                term = dot(dot_nt(spread, packed).astype(jnp.bfloat16), pick)
-            acc_ref[...] = acc_ref[...] + term
-    for r in range(1, 8):
-        touched = (node == lane_ref[pl.ds(base + r, 1), :]).astype(jnp.float32)
-        if side:
-            mask = 1.0 - lax.dot_general(
-                jnp.ones((8, 128), jnp.float32), touched, (((1,), (1,)), ((), ())), preferred_element_type=jnp.float32
-            )
-            block = acc_ref[pl.ds((r - 1) * CHUNK, CHUNK), :] * mask[0:1, :]
-            far_ref[pl.ds((r - 1) * CHUNK, CHUNK), :] = block.astype(jnp.bfloat16)
-        else:
-            mask = 1.0 - jnp.sum(touched, axis=1, keepdims=True)
-            block = acc_ref[:, pl.ds((r - 1) * CHUNK, CHUNK)] * mask
-            far_ref[:, pl.ds((r - 1) * CHUNK, CHUNK)] = block.astype(jnp.bfloat16)
-    if side:
-        own_ref[...] = acc_ref[pl.ds(FAR, CP), :].astype(jnp.bfloat16)
-    else:
-        own_ref[...] = acc_ref[:, pl.ds(FAR, CP)].astype(jnp.bfloat16)
+            spread = one_hot(node == lane_ref[pl.ds(16 + 8 * half + s, 1), :])
+            part = dot_nt(spread, packed).astype(jnp.bfloat16)
+            acc_ref[...] = acc_ref[...] + dot(part, chosen(table_ref, 8 + s, FACE * half, FACE))
+    for r in range(1, 8):
+        touched = (node == lane_ref[pl.ds(16 + r, 1), :]).astype(jnp.float32)
+        block = acc_ref[:, pl.ds((r - 1) * CHUNK, CHUNK)] * (1.0 - jnp.sum(touched, axis=1, keepdims=True))
+        far_ref[:, pl.ds((r - 1) * CHUNK, CHUNK)] = block.astype(jnp.bfloat16)
+    own_ref[...] = acc_ref[:, pl.ds(FAR, CP)].astype(jnp.bfloat16)
 
 
 def send_terms(me, corr_ref, coupling_ref, ham_ref, y, own_ref, c_ref, f_ref, send_ref):
@@ -462,14 +467,15 @@
     ax = swap(sx, 1)
     ay = swap(sy, 0)
     ownx, farx = call(
-        functools.partial(assemble_kernel, 1, FACE),
+        functools.partial(assemble_rows_kernel, FACE),
         me,
         (ax, betas, lanes, tables),
         [((CP, NODES), bf16), ((FAR, NODES), bf16)],
-        [((ROWS, NODES), f32)],
+        [((ROWS, NODES), f32), ((8 * CP, ROWS), bf16), ((8 * CP, NODES), f32)],
+        24 << 20,
     )
     owny, fary = call(
-        functools.partial(assemble_kernel, 0, 0),
+        functools.partial(assemble_columns_kernel, 0),
         me,
         (ay, turned, lanes, tables),
         [((NODES, CP), bf16), ((NODES, FAR), bf16)],

time: 213 us -> 212 us (level)
  the two profiles are of different devices: /device:TPU:1 before, /device:TPU:21 now
where the time goes in v5:
time: 212 us; the launch traced here: 211 us
  blocking collectives  139 us (66%)
  starting transfers between devices  30.1 us (14%)
  Pallas kernels  21.1 us (10%)
  waiting for transfers between devices  14.3 us (7%)
  local copies, waits for them, and re-layouts  5.33 us (3%)
    all_to_all x7, blocking collectives, swap(): lax.all_to_all(chunks, AXES, 0, 0, axis_index_groups=bricks(sizes, OFFSET...  139 us
    all_to_all x3, starting transfers between devices, swap(): lax.all_to_all(chunks, AXES, 0, 0, axis_index_groups=bricks(sizes, OFFSET...  30.1 us
    pallas_call x12, Pallas kernels, call(): pl.pallas_call(kernel, out_shape=[jax.ShapeDtypeStruct(shape, dtype) for...  21.1 us
    all_to_all x3, waiting for transfers between devices, swap(): lax.all_to_all(chunks, AXES, 0, 0, axis_index_groups=bricks(sizes, OFFSET...  14.3 us
    unnamed x33, local copies, waits for them, and re-layouts  4.9 us
  transfers between devices with their start and end apart: 3, of which 3 were waited for; matrix products, arithmetic and copies ran while one was open for 1% of the time, Pallas kernels for 4%

profile of v5, /device:TPU:21, one launch (start us, length us, event | category | flops | bytes accessed | tf_op | source)
XLA Modules:
  0.0 211.3 jit_solution(948031372058742811)
XLA Ops:
  0.0 3.2 %shard_map.100 = (bf16[144,392]{1,0:T(8,128)(2,1)}, bf16[392,144]{1,0:T(8,128)(2,1)}, bf16[392,128]{1,0:T(8,128)(2,1)}, f32[144,128]{1,0:T(8,128)}, f32[8,144,128]{2,1,0:T(8,128)}, /*index=5*/f32[8,72,128]{2,1,0:T(8,128)}) custom-call(s32[1]{0:T(128)} %bitcast.me_ref, bf16[18,8,343]{2,1,0:T(8,128)(2,1)} %bitcast.16, bf16[7,7,7,128]{3,2,1,0:T(8,128)(2,1)} %wave_ref.1, ...), custom_call_target="tpu_custom_call" | custom-call | tf_op jit(solution)/shard_map/pallas_call | solution.py:397
  3.2 4.5 %all-to-all-start.1 = ((f32[8,72,128]{2,1,0:T(8,128)}), f32[8,72,128]{2,1,0:T(8,128)S(1)}, u32[]{:S(2)}, u32[]{:S(2)}) async-start(f32[8,72,128]{2,1,0:T(8,128)} %get-tuple-element.37), calls=%async_computation.1 | async-start | bytes 589824 | tf_op jit(solution)/shard_map/all_to_all | solution.py:55
  8.5 3.8 %all-to-all-done.1.in_ref = f32[8,72,128]{2,1,0:T(8,128)S(1)} async-done(((f32[8,72,128]{2,1,0:T(8,128)}), f32[8,72,128]{2,1,0:T(8,128)S(1)}, u32[]{:S(2)}, u32[]{:S(2)}) %all-to-all-start.1) | async-done | bytes 294944 | tf_op jit(solution)/shard_map/all_to_all | solution.py:55
  12.3 19.2 %all-to-all-start = ((f32[8,144,128]{2,1,0:T(8,128)}), f32[8,144,128]{2,1,0:T(8,128)S(1)}, u32[]{:S(2)}, u32[]{:S(2)}) async-start(f32[8,144,128]{2,1,0:T(8,128)} %get-tuple-element.34), calls=%async_computation | async-start | bytes 1179648 | tf_op jit(solution)/shard_map/all_to_all | solution.py:55
  32.5 1.0 convolution_convert_fusion.ham_ref
  33.5 5.5 %shard_map.101 = (bf16[392,144]{1,0:T(8,128)(2,1)S(1)}, bf16[392,896]{1,0:T(8,128)(2,1)S(1)}) custom-call(s32[1]{0:T(128)} %bitcast.me_ref, f32[8,72,128]{2,1,0:T(8,128)S(1)} %all-to-all-done.1.in_ref, bf16[392,144]{1,0:T(8,128)(2,1)S(1)} %copy-done.7, s32[32,128]{1,0:T(8,128)S(1)} %copy-done.10, s32[16,1040]{1,0:T(8,128)S(1)} %copy-done.5), custom_call_target="tpu_custom_call" | custom-call | tf_op jit(solution)/shard_map/pallas_call | solution.py:397
  39.0 8.2 %all-to-all-done.in_ref = f32[8,144,128]{2,1,0:T(8,128)S(1)} async-done(((f32[8,144,128]{2,1,0:T(8,128)}), f32[8,144,128]{2,1,0:T(8,128)S(1)}, u32[]{:S(2)}, u32[]{:S(2)}) %all-to-all-start) | async-done | bytes 589856 | tf_op jit(solution)/shard_map/all_to_all | solution.py:55
  47.2 1.7 shard_map.102
  49.5 6.5 %all-to-all-start.2 = ((f32[8,128,128]{2,1,0:T(8,128)}), f32[8,128,128]{2,1,0:T(8,128)}, u32[]{:S(2)}, u32[]{:S(2)}) async-start(f32[8,128,128]{2,1,0:T(8,128)} %get-tuple-element.40), calls=%async_computation.2 | async-start | bytes 1048576 | tf_op jit(solution)/shard_map/all_to_all | solution.py:55
  57.8 2.5 %shard_map.103 = (bf16[144,392]{1,0:T(8,128)(2,1)S(1)}, bf16[896,392]{1,0:T(8,128)(2,1)S(1)}) custom-call(s32[1]{0:T(128)} %bitcast.me_ref, f32[8,144,128]{2,1,0:T(8,128)S(1)} %all-to-all-done.in_ref, bf16[144,392]{1,0:T(8,128)(2,1)S(1)} %copy-done.11, s32[32,128]{1,0:T(8,128)S(1)} %copy-done.10, s32[16,1040]{1,0:T(8,128)S(1)} %copy-done.6), custom_call_target="tpu_custom_call" | custom-call | tf_op jit(solution)/shard_map/pallas_call | solution.py:397
  60.9 2.3 %all-to-all-done.2.in_ref = f32[8,128,128]{2,1,0:T(8,128)} async-done(((f32[8,128,128]{2,1,0:T(8,128)}), f32[8,128,128]{2,1,0:T(8,128)}, u32[]{:S(2)}, u32[]{:S(2)}) %all-to-all-start.2) | async-done | bytes 524320 | tf_op jit(solution)/shard_map/all_to_all | solution.py:55
  63.2 0.9 copy-done.9
  64.2 1.9 shard_map.104
  66.1 30.1 %all_to_all.50.in_ref = f32[8,128,128]{2,1,0:T(8,128)S(1)} all-to-all(f32[8,128,128]{2,1,0:T(8,128)S(1)} %get-tuple-element.45), channel_id=1, replica_groups={{128,129,144,145,256,257,272,273},{130,131,146,147,258,259,274,275},{13..., dimensions={0} | all-to-all | bytes 1048576 | tf_op jit(solution)/shard_map/all_to_all | solution.py:55
  96.2 1.1 shard_map.105
  97.3 10.8 %all_to_all.51.in_ref = f32[8,128,128]{2,1,0:T(8,128)S(1)} all-to-all(f32[8,128,128]{2,1,0:T(8,128)S(1)} %get-tuple-element.48), channel_id=1, replica_groups={{17,18,33,34,145,146,161,162},{19,20,35,36,147,148,163,164},{21,22,37,3..., dimensions={0} | all-to-all | bytes 1048576 | tf_op jit(solution)/shard_map/all_to_all | solution.py:55
  109.0 22.1 %all_to_all.52.in_ref = f32[8,128,128]{2,1,0:T(8,128)S(1)} all-to-all(f32[8,128,128]{2,1,0:T(8,128)S(1)} %get-tuple-element.51), channel_id=1, replica_groups={{128,129,144,145,256,257,272,273},{130,131,146,147,258,259,274,275},{13..., dimensions={0} | all-to-all | bytes 1048576 | tf_op jit(solution)/shard_map/all_to_all | solution.py:55
  131.1 1.1 shard_map.107
  132.2 10.9 %all_to_all.53.in_ref = f32[8,128,128]{2,1,0:T(8,128)S(1)} all-to-all(f32[8,128,128]{2,1,0:T(8,128)S(1)} %get-tuple-element.53), channel_id=1, replica_groups={{17,18,33,34,145,146,161,162},{19,20,35,36,147,148,163,164},{21,22,37,3..., dimensions={0} | all-to-all | bytes 1048576 | tf_op jit(solution)/shard_map/all_to_all | solution.py:55
  144.0 17.3 %all_to_all.54.in_ref = f32[8,128,128]{2,1,0:T(8,128)S(1)} all-to-all(f32[8,128,128]{2,1,0:T(8,128)S(1)} %get-tuple-element.56), channel_id=1, replica_groups={{128,129,144,145,256,257,272,273},{130,131,146,147,258,259,274,275},{13..., dimensions={0} | all-to-all | bytes 1048576 | tf_op jit(solution)/shard_map/all_to_all | solution.py:55
  161.3 1.1 shard_map.109
  162.4 17.5 %all_to_all.55.in_ref = f32[8,128,128]{2,1,0:T(8,128)S(1)} all-to-all(f32[8,128,128]{2,1,0:T(8,128)S(1)} %get-tuple-element.58), channel_id=1, replica_groups={{17,18,33,34,145,146,161,162},{19,20,35,36,147,148,163,164},{21,22,37,3..., dimensions={0} | all-to-all | bytes 1048576 | tf_op jit(solution)/shard_map/all_to_all | solution.py:55
  180.4 30.0 %all_to_all.56.in_ref = f32[8,56,128]{2,1,0:T(8,128)S(1)} all-to-all(f32[8,56,128]{2,1,0:T(8,128)S(1)} %get-tuple-element.61), channel_id=1, replica_groups={{128,129,144,145,256,257,272,273},{130,131,146,147,258,259,274,275},{13..., dimensions={0} | all-to-all | bytes 458752 | tf_op jit(solution)/shard_map/all_to_all | solution.py:55
  210.4 1.0 shard_map.111
  (54 shorter events, 7.1 us)
Async XLA Ops:
  0.0 32.4 %copy-start = (bf16[1,1,1,343,343]{4,3,2,1,0:T(8,128)(2,1)S(1)}, bf16[1,1,1,343,343]{4,3,2,1,0:T(8,128)(2,1)}, u32[]{:S(2)}) copy-start(bf16[1,1,1,343,343]{4,3,2,1,0:T(8,128)(2,1)} %param.11) | copy-start | bytes 705898
  3.2 9.1 %all-to-all-start.1 = ((f32[8,72,128]{2,1,0:T(8,128)}), f32[8,72,128]{2,1,0:T(8,128)S(1)}, u32[]{:S(2)}, u32[]{:S(2)}) async-start(f32[8,72,128]{2,1,0:T(8,128)} %get-tuple-element.37), calls=%async_computation.1 | async-start | bytes 589824 | tf_op jit(solution)/shard_map/all_to_all | solution.py:55
  7.7 0.7 copy-start.15
  12.3 19.3 %copy-start.14 = (f32[2,18,18]{2,0,1:T(2,128)S(1)}, f32[2,18,18]{2,0,1:T(2,128)}, u32[]{:S(2)}) copy-start(f32[2,18,18]{2,0,1:T(2,128)} %param.14) | copy-start | bytes 7780
  12.3 34.9 %all-to-all-start = ((f32[8,144,128]{2,1,0:T(8,128)}), f32[8,144,128]{2,1,0:T(8,128)S(1)}, u32[]{:S(2)}, u32[]{:S(2)}) async-start(f32[8,144,128]{2,1,0:T(8,128)} %get-tuple-element.34), calls=%async_computation | async-start | bytes 1179648 | tf_op jit(solution)/shard_map/all_to_all | solution.py:55
  32.4 1.1 copy-start.5
  32.5 1.1 copy-start.7
  32.5 1.1 copy-start.10
  33.5 13.7 %copy-start.2 = (bf16[392,128]{1,0:T(8,128)(2,1)S(1)}, bf16[392,128]{1,0:T(8,128)(2,1)}, u32[]{:S(2)}) copy-start(bf16[392,128]{1,0:T(8,128)(2,1)} %get-tuple-element.36.y_ref.before_ref) | copy-start | bytes 301060
  33.5 13.7 %copy-start.13 = (f32[144,128]{1,0:T(8,128)S(1)}, f32[144,128]{1,0:T(8,128)}, u32[]{:S(2)}) copy-start(f32[144,128]{1,0:T(8,128)} %get-tuple-element.35.p_ref) | copy-start | bytes 221188
  48.9 0.7 copy-start.8
  49.5 13.7 %all-to-all-start.2 = ((f32[8,128,128]{2,1,0:T(8,128)}), f32[8,128,128]{2,1,0:T(8,128)}, u32[]{:S(2)}, u32[]{:S(2)}) async-start(f32[8,128,128]{2,1,0:T(8,128)} %get-tuple-element.40), calls=%async_computation.2 | async-start | bytes 1048576 | tf_op jit(solution)/shard_map/all_to_all | solution.py:55
  56.0 0.9 copy-start.6
  56.9 0.9 copy-start.11
  57.8 5.4 %copy-start.1 = (f32[392,1]{1,0:T(8,128)S(1)}, f32[392,1]{1,0:T(8,128)}, u32[]{:S(2)}) copy-start(f32[392,1]{1,0:T(8,128)} %constant.138.clone.share_ref) | copy-start | bytes 4708
  60.3 0.7 copy-start.3
  63.2 0.9 copy-start.9
  66.1 30.1 %copy-start.4 = (bf16[144,392]{1,0:T(8,128)(2,1)S(1)}, bf16[144,392]{1,0:T(8,128)(2,1)}, u32[]{:S(2)}) copy-start(bf16[144,392]{1,0:T(8,128)(2,1)} %copy-done.3) | copy-start | bytes 338692
  180.4 30.0 %copy-start.12 = (s32[16,392]{1,0:T(8,128)S(1)}, s32[16,392]{1,0:T(8,128)}, u32[]{:S(2)}) copy-start(s32[16,392]{1,0:T(8,128)} %constant.134.clone.perm_ref) | copy-start | bytes 75268
